TPU v7x, 32 devices: a whole 2x2x4 slice. The times are simulated.
32 devices in a mesh: row: 16 (over z, x, core), col: 2 (over y).
Axes of the slice: x: 2, y: 2, z: 4, core: 2. Of those that a mesh axis runs over, the one named last changes fastest.
Arguments:
- density_factor: bfloat16 [6144, 512], P('row', 'col'), may hold values from -0.25 to 0.25
- hole_factor: bfloat16 [6144, 512], P('row', 'col'), may hold values from -0.25 to 0.25
- ph_factor: bfloat16 [6144, 512], P('row', 'col'), may hold values from -0.25 to 0.25
- hamiltonian: bfloat16 [6144, 6144], P('row', 'col'), as said below
- multiplier_q: bfloat16 [6144, 6144], P('row', 'col'), as said below
- multiplier_g: bfloat16 [6144, 6144], P('row', 'col'), as said below
- ph_perm: int32 [6144], replicated, may hold values from 0 to 6143, as said below
- block_lengths: int32 [48], replicated, may hold values from 1 to 256, 6144 in all
Outputs:
- grad_density: float32 [6144, 512], P('row', 'col')
- grad_hole: float32 [6144, 512], P('row', 'col')
- grad_ph: float32 [6144, 512], P('row', 'col')
Inputs may be any that keep to these rules, and one draw needn't show every extreme that they name: `ph_perm`: a permutation of the rows; each aligned block of 384 entries holds exactly 24 values from each aligned range of 384 rows. `block_lengths`: the lengths sum to 6144. `hamiltonian`: symmetric. `multiplier_q`: symmetric. `multiplier_g`: symmetric.
All inputs are finite; a program needn't handle non-finite values.
Results may differ from a plain program's by a relative error of at most 0.00035.
The roundings to bfloat16 on the way count: a program that leaves them out, or rounds other values in their place, can miss the bound.
Values may be sent and summed in bfloat16 or wider, within the bound.
A program may use at most 128 MiB of HBM per device.

v0:
```python
import jax
import jax.numpy as jnp
from jax import lax
from jax.sharding import PartitionSpec as P

shift_value = 2.0
penalty = 2.5


def block_means(values, lengths):
    offsets = jnp.cumsum(lengths)
    positions = jnp.arange(values.shape[0], dtype=jnp.int32)
    segment = jnp.sum((positions[:, None] >= offsets[None, :]).astype(jnp.int32), axis=1)
    member = (segment[:, None] == jnp.arange(lengths.shape[0], dtype=jnp.int32)[None, :]).astype(
        jnp.float32
    )
    means = jnp.sum(member * values[:, None], axis=0) / lengths.astype(jnp.float32)
    return jnp.sum(member * means[None, :], axis=1)


def contract_rows(left, right):
    return lax.dot_general(
        left, right, (((1,), (1,)), ((), ())), preferred_element_type=jnp.float32
    )


def local(
    density_factor,
    hole_factor,
    ph_factor,
    hamiltonian,
    multiplier_q,
    multiplier_g,
    ph_perm,
    block_lengths,
):
    groups = lax.axis_size("row")
    col_groups = lax.axis_size("col")
    row_index = lax.axis_index("row")
    col_index = lax.axis_index("col")
    block = density_factor.shape[0]
    rank_part = density_factor.shape[1]
    width = multiplier_q.shape[1]
    sends = block // groups
    row_ids = row_index * block + jnp.arange(block, dtype=jnp.int32)
    col_ids = col_index * width + jnp.arange(width, dtype=jnp.int32)
    on_diag = row_ids[:, None] == col_ids[None, :]
    density_sq = jnp.sum(jnp.square(density_factor.astype(jnp.float32)), axis=1)
    ph_sq = jnp.sum(jnp.square(ph_factor.astype(jnp.float32)), axis=1)
    mult_diag = jnp.sum(jnp.where(on_diag, multiplier_g.astype(jnp.float32), 0.0), axis=1)
    density_sq, ph_sq, mult_diag = lax.psum((density_sq, ph_sq, mult_diag), "col")
    density_all, ph_all, mult_all = (
        lax.all_gather(density_sq, "row", axis=0, tiled=True),
        lax.all_gather(ph_sq, "row", axis=0, tiled=True),
        lax.all_gather(mult_diag, "row", axis=0, tiled=True),
    )
    shifted = 2.0 * block_means(density_all, block_lengths)
    shifted_ph = jnp.take(shifted, ph_perm)
    weight_diag = mult_all + penalty * (shifted_ph - jnp.take(density_all, ph_perm) - ph_all)
    weight_pair = jnp.zeros_like(weight_diag).at[ph_perm].set(weight_diag)
    scaling = 2.0 * block_means(weight_pair, block_lengths)
    scale_rows = lax.dynamic_slice_in_dim(scaling, row_index * block, block)
    shift_rows = lax.dynamic_slice_in_dim(shifted_ph, row_index * block, block)
    table = ph_perm.reshape(groups, block)
    source = table // block
    mine = lax.dynamic_index_in_dim(source, row_index, 0, keepdims=False)
    member = (mine[:, None] == jnp.arange(groups, dtype=jnp.int32)[None, :]).astype(jnp.int32)
    earlier = jnp.cumsum(member, axis=0) - member
    slot = mine * sends + jnp.sum(earlier * member, axis=1)
    slot_back = jnp.argsort(slot)
    position = jnp.arange(block, dtype=jnp.int32)[None, :]
    ranked = jnp.where(source == row_index, position, block + position)
    chosen = jnp.argsort(ranked, axis=1)[:, :sends]
    anchor = (jnp.take_along_axis(table, chosen, axis=1) - row_index * block).reshape(block)
    anchor_back = jnp.argsort(anchor)
    pair_local = jnp.concatenate([density_factor, hole_factor], axis=1)
    outgoing = jnp.take(density_factor, anchor, axis=0)
    incoming = lax.all_to_all(outgoing, "row", split_axis=0, concat_axis=0, tiled=True)
    density_ph = jnp.take(incoming, slot, axis=0)
    ph_local = jnp.concatenate([density_ph, ph_factor], axis=1)
    pair_whole, ph_whole = (
        lax.all_gather(pair_local, "row", axis=0, tiled=True),
        lax.all_gather(ph_local, "row", axis=0, tiled=True),
    )
    pair_cols, ph_cols = (
        lax.all_to_all(pair_whole, "col", split_axis=0, concat_axis=1, tiled=True),
        lax.all_to_all(ph_whole, "col", split_axis=0, concat_axis=1, tiled=True),
    )
    pair_full, ph_full = (
        lax.all_gather(pair_local, "col", axis=1, tiled=True),
        lax.all_gather(ph_local, "col", axis=1, tiled=True),
    )
    resid_q = jnp.where(on_diag, shift_value, 0.0) - contract_rows(pair_full, pair_cols)
    resid_g = jnp.where(on_diag, shift_rows[:, None], 0.0) - contract_rows(ph_full, ph_cols)
    weight_q = (multiplier_q.astype(jnp.float32) + penalty * resid_q).astype(jnp.bfloat16)
    weight_g = (multiplier_g.astype(jnp.float32) + penalty * resid_g).astype(jnp.bfloat16)
    weight_q, weight_g = (weight_q, weight_g)
    split_cols = pair_cols.reshape(width, col_groups, 2, rank_part)
    energy = jnp.einsum(
        "rc,cgk->rgk", hamiltonian, split_cols[:, :, 0, :], preferred_element_type=jnp.float32
    )
    pair_term = jnp.dot(weight_q, pair_cols, preferred_element_type=jnp.float32).reshape(
        block, col_groups, 2, rank_part
    )
    combined = jnp.stack(
        [2.0 * energy - 2.0 * pair_term[:, :, 0, :], -2.0 * pair_term[:, :, 1, :]], axis=2
    ).reshape(block, col_groups * 2 * rank_part)
    ph_term = jnp.dot(weight_g, ph_cols, preferred_element_type=jnp.float32)
    pair_grad, ph_acc = (
        lax.psum_scatter(combined, "col", scatter_dimension=1, tiled=True),
        lax.psum_scatter(ph_term, "col", scatter_dimension=1, tiled=True),
    )
    outgoing_back = jnp.take(ph_acc[:, :rank_part], slot_back, axis=0)
    returned = lax.all_to_all(outgoing_back, "row", split_axis=0, concat_axis=0, tiled=True)
    returned = jnp.take(returned, anchor_back, axis=0)
    grad_density = (
        pair_grad[:, :rank_part]
        + 2.0 * scale_rows[:, None] * density_factor.astype(jnp.float32)
        - 2.0 * returned
    )
    grad_hole = pair_grad[:, rank_part:]
    grad_ph = -2.0 * ph_acc[:, rank_part:]
    return (grad_density, grad_hole, grad_ph)


def solution(mesh):
    return jax.shard_map(
        local,
        mesh=mesh,
        in_specs=(
            P("row", "col"),
            P("row", "col"),
            P("row", "col"),
            P("row", "col"),
            P("row", "col"),
            P("row", "col"),
            P(),
            P(),
        ),
        out_specs=(P("row", "col"), P("row", "col"), P("row", "col")),
        check_vma=False,
    )
```

profile of v0, /device:TPU:0, one launch (start us, length us, event | category | flops | bytes accessed | tf_op | source)
XLA Modules:
  0.0 450.4 jit_solution(13643804894976659975)
XLA Ops:
  7.2 0.9 reshape.128
  8.1 0.6 add_select_fusion
  8.8 0.6 iota.52
  9.5 0.9 reduce-window.19
  10.3 0.2 slice_reduce_fusion
  10.6 0.1 fusion.32
  10.7 3.2 sort.52.cloned.1.call-done
  13.9 0.7 bitcast_or_fusion
  14.6 0.1 reshape.179
  14.7 3.4 gather_fusion
  18.3 0.7 select_subtract_fusion.1
  19.0 0.1 sub.41
  19.1 2.1 gather_fusion.3
  21.2 0.8 broadcast_select_fusion.2
  22.0 7.4 %all-to-all-start.1 = ((bf16[16,24,256]{2,1,0:T(8,128)(2,1)}), bf16[16,24,256]{2,1,0:T(8,128)(2,1)S(1)}, u32[]{:S(2)}, u32[]{:S(2)}) async-start(bf16[16,24,256]{2,1,0:T(8,128)(2,1)} %bitcast.19), calls=%async_computation.2 | async-start | bytes 393216 | tf_op jit(solution)/shard_map/all_to_all | solution.py:78
  29.5 8.9 %all-to-all-done.1 = bf16[16,24,256]{2,1,0:T(8,128)(2,1)S(1)} async-done(((bf16[16,24,256]{2,1,0:T(8,128)(2,1)}), bf16[16,24,256]{2,1,0:T(8,128)(2,1)S(1)}, u32[]{:S(2)}, u32[]{:S(2)}) %all-to-all-start.1) | async-done | bytes 196640 | tf_op jit(solution)/shard_map/all_to_all | solution.py:78
  38.3 2.0 gather_fusion.4
  40.4 0.1 broadcast_select_fusion.1
  40.5 0.8 pad_maximum_fusion.1
  41.4 0.9 constant_dynamic-update-slice_fusion
  42.4 0.7 copy-done.3
  43.1 57.7 %all-gather.8.cloned.1.call-done = bf16[6144,512]{1,0:T(8,128)(2,1)} async-done(((bf16[384,512]{1,0:T(8,128)(2,1)}), bf16[6144,512]{1,0:T(8,128)(2,1)}) %all-gather.8.cloned.1.call-update) | async-done | bytes 6291472 | tf_op jit(solution)/shard_map/all_gather | solution.py:83
  100.8 8.7 %copy.61 = bf16[2,3072,512]{1,2,0:T(8,128)(2,1)} copy(bf16[2,3072,512]{2,1,0:T(8,128)(2,1)} %bitcast.96) | data formatting | bytes 12582912 | tf_op jit(solution)/shard_map/all_to_all | solution.py:87
  109.5 6.3 %all-to-all-start.2 = ((bf16[2,3072,512]{1,2,0:T(8,128)(2,1)}), bf16[2,3072,512]{1,2,0:T(8,128)(2,1)}, u32[]{:S(2)}, u32[]{:S(2)}) async-start(bf16[2,3072,512]{1,2,0:T(8,128)(2,1)} %copy.61), calls=%async_computation.3 | async-start | bytes 12582912 | tf_op jit(solution)/shard_map/all_to_all | solution.py:87
  115.8 0.1 fusion.27
  116.0 0.2 multiply_reduce_fusion
  116.1 2.4 fusion.7
  118.6 67.9 %all-reduce = (f32[384]{0:T(512)S(1)}, f32[384]{0:T(512)S(1)}, f32[384]{0:T(512)S(1)}) all-reduce(f32[384]{0:T(512)S(1)} %fusion.27, f32[384]{0:T(512)S(1)} %fusion.7, f32[384]{0:T(512)S(1)} %multiply_reduce_fusion), channel_id=1, replica_groups=mesh['row'=16,'col'=2] {'col'}, use_global_device_ids=true, to_apply=%region_6.7 | all-reduce | flops 1152 | bytes 9216 | tf_op jit(solution)/shard_map/psum | solution.py:51
  186.5 0.1 copy.59
  186.6 0.1 reduce
  186.7 19.4 %all-gather.1 = f32[16,1,384]{2,1,0:T(1,128)S(1)} all-gather(f32[1,1,384]{2,1,0:T(1,128)S(1)} %reshape.207), channel_id=1, replica_groups=mesh['row'=16,'col'=2] {'row'}, dimensions={0}, use_global_device_ids=true | all-gather | bytes 26112 | tf_op jit(solution)/shard_map/all_gather | solution.py:53
  206.1 0.2 convert_reduce_fusion
  206.4 6.3 %all-to-all-start = ((bf16[2,3072,512]{2,1,0:T(8,128)(2,1)}), bf16[2,3072,512]{2,1,0:T(8,128)(2,1)}, u32[]{:S(2)}, u32[]{:S(2)}) async-start(bf16[2,3072,512]{2,1,0:T(8,128)(2,1)} %bitcast.95), calls=%async_computation | async-start | bytes 12582912 | tf_op jit(solution)/shard_map/all_to_all | solution.py:86
  212.8 0.3 select_reduce_fusion.3
  213.0 34.3 %gather_fusion.2 = f32[6144]{0:T(1024)S(1)} fusion(f32[6144]{0:T(1024)S(1)} %bitcast.92, s32[6144]{0:T(1024)S(1)} %get-tuple-element.24), kind=kCustom, calls=%fused_computation.3.clone | custom fusion | bytes 73728 | tf_op jit(solution)/shard_map/jit(_take)/gather | solution.py:59
  247.3 0.3 select_reduce_fusion.2
  247.6 34.3 %gather_fusion.1 = f32[6144]{0:T(1024)S(1)} fusion(f32[6144]{0:T(1024)S(1)} %broadcast_multiply_fusion, s32[6144]{0:T(1024)S(1)} %get-tuple-element.24), kind=kCustom, calls=%fused_computation.clone | custom fusion | bytes 73728 | tf_op jit(solution)/shard_map/jit(_take)/gather | solution.py:58
  281.9 17.5 %all-gather = f32[16,1,384]{2,1,0:T(1,128)S(1)} all-gather(f32[1,1,384]{2,1,0:T(1,128)S(1)} %reshape.205), channel_id=1, replica_groups=mesh['row'=16,'col'=2] {'row'}, dimensions={0}, use_global_device_ids=true | all-gather | bytes 26112 | tf_op jit(solution)/shard_map/all_gather | solution.py:55
  299.4 18.8 %all-gather.2 = f32[16,1,384]{2,1,0:T(1,128)S(1)} all-gather(f32[1,1,384]{2,1,0:T(1,128)S(1)} %reshape.209), channel_id=1, replica_groups=mesh['row'=16,'col'=2] {'row'}, dimensions={0}, use_global_device_ids=true | all-gather | bytes 26112 | tf_op jit(solution)/shard_map/all_gather | solution.py:54
  318.3 0.1 dynamic_slice.11
  318.4 12.3 %all_gather.26 = bf16[384,1024]{1,0:T(8,128)(2,1)} all-gather(bf16[384,512]{1,0:T(8,128)(2,1)S(1)} %copy-done.2), channel_id=1, replica_groups=mesh['row'=16,'col'=2] {'col'}, dimensions={1}, use_global_device_ids=true | all-gather | bytes 1179648 | tf_op jit(solution)/shard_map/all_gather | solution.py:91
  330.7 12.1 %fusion.25 = f32[384,1024]{1,0:T(8,128)} fusion(bf16[3072,1024]{0,1:T(8,128)(2,1)} %bitcast.23, bf16[384,3072]{1,0:T(8,128)(2,1)} %param.19, bf16[384,1024]{1,0:T(8,128)(2,1)} %all_gather.26, f32[384]{0:T(512)S(1)} %dynamic_slice.11, s32[3072]{0:T(1024)S(1)} %iota_add_fusion, s32[384]{0:T(512)S(1)} %iota_add_fusion.2), kind=kOutput, calls=%fused_computation.38 | convolution fusion | flops 4840095744 | bytes 11025408 | tf_op jit(solution)/shard_map/dot_general | solution.py:108
  342.8 0.2 reduce-scatter.3.cloned.1.call-start
  343.1 18.9 %all_gather.22 = bf16[384,1024]{1,0:T(8,128)(2,1)} all-gather(bf16[384,512]{1,0:T(8,128)(2,1)S(1)} %copy-done.4), channel_id=1, replica_groups=mesh['row'=16,'col'=2] {'col'}, dimensions={1}, use_global_device_ids=true | all-gather | bytes 1179648 | tf_op jit(solution)/shard_map/all_gather | solution.py:90
  362.0 8.8 %copy.52 = bf16[3072,2,512]{0,2,1:T(8,128)(2,1)} copy(bf16[3072,2,512]{2,0,1:T(8,128)(2,1)} %bitcast.1) | data formatting | bytes 12582912 | tf_op jit(solution)/shard_map/all_to_all | solution.py:86
  370.7 12.5 %fusion = f32[384,2,2,256]{0,3,1,2:T(8,128)} fusion(bf16[2,2,256,3072]{3,2,1,0:T(8,128)(2,1)} %bitcast.97, bf16[384,1024]{1,0:T(8,128)(2,1)S(1)} %copy-done.5, bf16[3072,1024]{0,1:T(8,128)(2,1)} %bitcast.98, bf16[384,3072]{1,0:T(8,128)(2,1)} %param.18, s32[3072]{0:T(1024)S(1)} %iota_add_fusion, s32[384]{0:T(512)S(1)} %iota_add_fusion.2), kind=kOutput, calls=%fused_computation.11 | convolution fusion | flops 4840095744 | bytes 17315328 | tf_op jit(solution)/shard_map/dot_general | solution.py:102
  383.3 1.2 slice_multiply_fusion
  384.5 3.9 fusion.22
  388.4 0.1 pad_maximum_fusion
  388.5 1.2 copy.57
  389.7 3.0 copy.58
  392.8 3.8 sort.49
  396.6 23.0 %scatter_custom_fusion = f32[6144]{0:T(1024)S(1)} fusion(s32[6144]{0:T(1024)S(1)} %get-tuple-element.23, f32[6144]{0:T(1024)S(1)} %get-tuple-element.15, f32[]{:T(128)} %constant.60.clone.1), kind=kCustom, calls=%fused_computation.78 | custom fusion | bytes 24580 | tf_op jit(solution)/shard_map/scatter | solution.py:60
  419.6 0.3 select_reduce_fusion.1
  419.9 1.9 slice_multiply_fusion.2
  421.8 1.7 gather_fusion.5
  423.5 0.9 broadcast_select_fusion
  424.4 3.6 all-to-all-start.3
  427.9 0.3 select_reduce_fusion
  428.2 0.1 fusion.40
  428.3 3.8 sort.50
  432.1 8.0 %all-to-all-done.3 = f32[16,24,256]{2,1,0:T(8,128)S(1)} async-done(((f32[16,24,256]{2,1,0:T(8,128)}), f32[16,24,256]{2,1,0:T(8,128)S(1)}, u32[]{:S(2)}, u32[]{:S(2)}) %all-to-all-start.3) | async-done | bytes 393248 | tf_op jit(solution)/shard_map/all_to_all | solution.py:114
  440.1 1.7 gather_fusion.6
  441.8 2.1 fusion.46
  (63 shorter events, 0.8 us)
Async XLA Ops:
  7.2 377.3 %copy-start = (bf16[384,3072]{1,0:T(8,128)(2,1)S(1)}, bf16[384,3072]{1,0:T(8,128)(2,1)}, u32[]{:S(2)}) copy-start(bf16[384,3072]{1,0:T(8,128)(2,1)} %param.17) | copy-start | bytes 7077892
  7.2 6.7 %sort.52.cloned.1.call-start = ((), (), s32[]{:S(2)}) async-start(), calls=%async_computation.10 | async-start | bytes 147488 | tf_op jit(solution)/shard_map/jit(argsort)/sort | solution.py:73
  14.7 4.4 copy-start.1
  19.1 21.4 %copy-start.6 = (bf16[384,256]{1,0:T(8,128)(2,1)S(1)}, bf16[384,256]{1,0:T(8,128)(2,1)}, u32[]{:S(2)}) copy-start(bf16[384,256]{1,0:T(8,128)(2,1)} %param.16) | copy-start | bytes 589828
  22.0 16.4 %all-to-all-start.1 = ((bf16[16,24,256]{2,1,0:T(8,128)(2,1)}), bf16[16,24,256]{2,1,0:T(8,128)(2,1)S(1)}, u32[]{:S(2)}, u32[]{:S(2)}) async-start(bf16[16,24,256]{2,1,0:T(8,128)(2,1)} %bitcast.19), calls=%async_computation.2 | async-start | bytes 393216 | tf_op jit(solution)/shard_map/all_to_all | solution.py:78
  29.4 71.5 %all-gather.8.cloned.1.call-start = ((), (), s32[]{:S(2)}) async-start(), calls=%async_computation.8 | async-start | bytes 6684672 | tf_op jit(solution)/shard_map/all_gather | solution.py:83
  41.3 165.0 %all-gather.6.cloned.1.call-start = ((), (), s32[]{:S(2)}) async-start(), calls=%async_computation.6 | async-start | bytes 6684672 | tf_op jit(solution)/shard_map/all_gather | solution.py:82
  42.4 0.7 copy-start.3
  109.5 96.9 %all-to-all-start.2 = ((bf16[2,3072,512]{1,2,0:T(8,128)(2,1)}), bf16[2,3072,512]{1,2,0:T(8,128)(2,1)}, u32[]{:S(2)}, u32[]{:S(2)}) async-start(bf16[2,3072,512]{1,2,0:T(8,128)(2,1)} %copy.61), calls=%async_computation.3 | async-start | bytes 12582912 | tf_op jit(solution)/shard_map/all_to_all | solution.py:87
  115.8 70.7 %copy-start.8 = (s32[48]{0:T(128)S(1)}, s32[48]{0:T(128)}, u32[]{:S(2)}) copy-start(s32[48]{0:T(128)} %param.21) | copy-start | bytes 580
  115.8 90.5 %copy-start.7 = (s32[6144]{0:T(1024)S(1)}, s32[6144]{0:T(1024)}, u32[]{:S(2)}) copy-start(s32[6144]{0:T(1024)} %param.20) | copy-start | bytes 73732
  206.4 155.6 %all-to-all-start = ((bf16[2,3072,512]{2,1,0:T(8,128)(2,1)}), bf16[2,3072,512]{2,1,0:T(8,128)(2,1)}, u32[]{:S(2)}, u32[]{:S(2)}) async-start(bf16[2,3072,512]{2,1,0:T(8,128)(2,1)} %bitcast.95), calls=%async_computation | async-start | bytes 12582912 | tf_op jit(solution)/shard_map/all_to_all | solution.py:86
  212.7 207.2 %reduce-scatter.5.cloned.1.call-start = ((), (), s32[]{:S(2)}) async-start(), calls=%async_computation.9 | async-start | bytes 2359296 | tf_op jit(solution)/shard_map/reduce_scatter | solution.py:111
  247.6 70.7 %copy-start.2 = (bf16[384,512]{1,0:T(8,128)(2,1)S(1)}, bf16[384,512]{1,0:T(8,128)(2,1)}, u32[]{:S(2)}) copy-start(bf16[384,512]{1,0:T(8,128)(2,1)} %pad_maximum_fusion.1) | copy-start | bytes 1179652
  330.7 12.4 %copy-start.4 = (bf16[384,512]{1,0:T(8,128)(2,1)S(1)}, bf16[384,512]{1,0:T(8,128)(2,1)}, u32[]{:S(2)}) copy-start(bf16[384,512]{1,0:T(8,128)(2,1)} %copy-done.3) | copy-start | bytes 1179652
  342.8 98.9 %reduce-scatter.3.cloned.1.call-start = ((), (), s32[]{:S(2)}) async-start(), calls=%async_computation.7 | async-start | bytes 2359296 | tf_op jit(solution)/shard_map/reduce_scatter | solution.py:110
  362.0 8.8 %copy-start.5 = (bf16[384,1024]{1,0:T(8,128)(2,1)S(1)}, bf16[384,1024]{1,0:T(8,128)(2,1)}, u32[]{:S(2)}) copy-start(bf16[384,1024]{1,0:T(8,128)(2,1)} %all_gather.22) | copy-start | bytes 2359300
  424.4 15.7 %all-to-all-start.3 = ((f32[16,24,256]{2,1,0:T(8,128)}), f32[16,24,256]{2,1,0:T(8,128)S(1)}, u32[]{:S(2)}, u32[]{:S(2)}) async-start(f32[16,24,256]{2,1,0:T(8,128)} %bitcast.101), calls=%async_computation.5 | async-start | bytes 786432 | tf_op jit(solution)/shard_map/all_to_all | solution.py:114
Sparse Core Ops, SparseCore 0:
  11.0 2.6 sort.54.cloned.1.call-done
  41.5 59.3 all-gather.7
  103.7 60.0 all-gather.5
  343.0 29.6 reduce-scatter.4
  392.9 24.4 reduce-scatter.2
  (1 shorter events, 0.0 us)
where the time goes:
time: 452 us; the launch traced here: 450 us
  blocking collectives  155 us (34%)
  local copies, waits for them, and re-layouts  131 us (29%)
  waiting for transfers between devices  74.7 us (17%)
  matrix products  28.6 us (6%)
  starting transfers between devices  23.9 us (5%)
  other arithmetic  22.9 us (5%)
  between operations  14.2 us (3%)
    psum x1, blocking collectives, local(): lax.psum((density_sq, ph_sq, mult_diag), 'col')  67.9 us
    all_gather x1, waiting for transfers between devices, local(): lax.all_gather(ph_local, 'row', axis=0, tiled=True)  57.7 us
    gather x1, local copies, waits for them, and re-layouts, local(): shifted_ph = jnp.take(shifted, ph_perm)  34.3 us
    gather x1, local copies, waits for them, and re-layouts, local(): jnp.take(density_all, ph_perm)  34.3 us
    scatter x1, local copies, waits for them, and re-layouts, local(): weight_pair = jnp.zeros_like(weight_diag).at[ph_perm].set(weight_diag)  23 us
    all_gather x1, blocking collectives, local(): lax.all_gather(density_sq, 'row', axis=0, tiled=True)  19.4 us
    all_gather x1, blocking collectives, local(): lax.all_gather(pair_local, 'col', axis=1, tiled=True)  18.9 us
    all_gather x1, blocking collectives, local(): lax.all_gather(ph_sq, 'row', axis=0, tiled=True)  18.8 us
  transfers between devices with their start and end apart: 8, of which 3 were waited for; matrix products, arithmetic and copies ran while one was open for 36% of the time, Pallas kernels for 0%

commit v1 on v0

v1 whole, which is shorter than its diff:
```python
import jax
import jax.numpy as jnp
from jax import lax
from jax.experimental import pallas as pl
from jax.experimental.pallas import tpu as pltpu
from jax.sharding import PartitionSpec as P

shift_value = 2.0
penalty = 2.5


def tile_weight(offset_ref, own_ref, cols_ref, mult_ref, shift):
    parts, block, _ = own_ref.shape
    tile = cols_ref.shape[1]
    gram = None
    for part in range(parts):
        term = lax.dot_general(
            own_ref[part],
            cols_ref[part],
            (((1,), (1,)), ((), ())),
            preferred_element_type=jnp.float32,
        )
        gram = term if gram is None else gram + term
    rows = lax.broadcasted_iota(jnp.int32, (block, tile), 0) + offset_ref[0]
    cols = lax.broadcasted_iota(jnp.int32, (block, tile), 1) + pl.program_id(0) * tile
    resid = jnp.where(rows == cols, shift, 0.0) - gram
    return (mult_ref[...].astype(jnp.float32) + penalty * resid).astype(jnp.bfloat16)


def pair_kernel(offset_ref, own_ref, cols_ref, mult_ref, ham_ref, out_ref):
    @pl.when(pl.program_id(0) == 0)
    def _():
        out_ref[...] = jnp.zeros_like(out_ref)

    half = own_ref.shape[2] // 2
    weight = tile_weight(offset_ref, own_ref, cols_ref, mult_ref, shift_value)
    for part in range(own_ref.shape[0]):
        first = cols_ref[part, :, :half]
        out_ref[part, :, :half] += jnp.dot(
            ham_ref[...], first, preferred_element_type=jnp.float32
        ) - jnp.dot(weight, first, preferred_element_type=jnp.float32)
        out_ref[part, :, half:] -= jnp.dot(
            weight, cols_ref[part, :, half:], preferred_element_type=jnp.float32
        )


def ph_kernel(offset_ref, own_ref, cols_ref, mult_ref, shift_ref, out_ref):
    @pl.when(pl.program_id(0) == 0)
    def _():
        out_ref[...] = jnp.zeros_like(out_ref)

    weight = tile_weight(offset_ref, own_ref, cols_ref, mult_ref, shift_ref[...])
    for part in range(own_ref.shape[0]):
        out_ref[part] -= jnp.dot(weight, cols_ref[part], preferred_element_type=jnp.float32)


def apply_weight(kernel, name, offset, own, cols, mult, extra, extra_tiled):
    parts, block, depth = own.shape
    width = cols.shape[1]
    tile = 512 if width % 512 == 0 else 256
    if extra_tiled:
        extra_spec = pl.BlockSpec((block, tile), lambda j, o: (0, j))
    else:
        extra_spec = pl.BlockSpec(extra.shape, lambda j, o: (0, 0))
    return pl.pallas_call(
        kernel,
        name=name,
        out_shape=jax.ShapeDtypeStruct((parts, block, depth), jnp.float32),
        grid_spec=pltpu.PrefetchScalarGridSpec(
            num_scalar_prefetch=1,
            grid=(width // tile,),
            in_specs=[
                pl.BlockSpec((parts, block, depth), lambda j, o: (0, 0, 0)),
                pl.BlockSpec((parts, tile, depth), lambda j, o: (0, j, 0)),
                pl.BlockSpec((block, tile), lambda j, o: (0, j)),
                extra_spec,
            ],
            out_specs=pl.BlockSpec((parts, block, depth), lambda j, o: (0, 0, 0)),
        ),
        compiler_params=pltpu.CompilerParams(
            dimension_semantics=("arbitrary",), vmem_limit_bytes=40 << 20
        ),
        cost_estimate=pl.CostEstimate(
            flops=(5 if extra_tiled else 4) * block * width * parts * depth,
            bytes_accessed=2 * width * (parts * depth + 2 * block),
            transcendentals=0,
        ),
    )(offset, own, cols, mult, extra)


def select(one_hot, values, left_axis):
    if values.dtype == jnp.float32:
        precision = lax.Precision.HIGHEST
    else:
        precision = None
    return lax.dot_general(
        one_hot.astype(values.dtype),
        values,
        (((left_axis,), (0,)), ((), ())),
        precision=precision,
        preferred_element_type=jnp.float32,
    ).astype(values.dtype)


def local(
    density_factor,
    hole_factor,
    ph_factor,
    hamiltonian,
    multiplier_q,
    multiplier_g,
    ph_perm,
    block_lengths,
):
    groups = lax.axis_size("row")
    col_groups = lax.axis_size("col")
    row_index = lax.axis_index("row")
    col_index = lax.axis_index("col")
    block, rank_part = density_factor.shape
    width = multiplier_q.shape[1]
    sends = block // groups
    per = groups // col_groups
    both = ("row", "col")

    placing = [
        (r * col_groups + c, (c * per + r % per) * col_groups + r // per)
        for r in range(groups)
        for c in range(col_groups)
    ]

    def whole_cols(piece):
        placed = lax.ppermute(piece, both, placing)
        whole = lax.all_gather(placed, "row", axis=0, tiled=True)
        return whole.reshape(col_groups, width, 2 * rank_part)

    pair_local = jnp.concatenate([density_factor, hole_factor], axis=1)
    pair_cols = whole_cols(pair_local)

    index = jnp.arange(block, dtype=jnp.int32)
    row_ids = row_index * block + index
    mine = lax.dynamic_slice_in_dim(ph_perm, row_index * block, block)
    source = mine // block
    same_source = (source[:, None] == source[None, :]) & (index[None, :] < index[:, None])
    slot = source * sends + jnp.sum(same_source.astype(jnp.int32), axis=1)
    everywhere = jnp.arange(groups * block, dtype=jnp.int32)
    inverse = jnp.sum(
        jnp.where(ph_perm[None, :] == row_ids[:, None], everywhere[None, :], 0), axis=1
    )
    target = inverse // block
    same_target = (target[:, None] == target[None, :]) & (inverse[None, :] < inverse[:, None])
    outlet = target * sends + jnp.sum(same_target.astype(jnp.int32), axis=1)
    send_hot = outlet[:, None] == index[None, :]
    take_hot = slot[:, None] == index[None, :]

    outgoing = select(send_hot, density_factor, 0)
    incoming = lax.all_to_all(outgoing, "row", split_axis=0, concat_axis=0, tiled=True)
    density_ph = select(take_hot, incoming, 1)
    ph_local = jnp.concatenate([density_ph, ph_factor], axis=1)
    ph_cols = whole_cols(ph_local)

    lengths = block_lengths.astype(jnp.float32)
    count = block_lengths.shape[0]
    upto = jnp.arange(count, dtype=jnp.int32)
    ends = jnp.sum(jnp.where(upto[None, :] <= upto[:, None], block_lengths[None, :], 0), axis=1)
    starts = ends - block_lengths

    def member_of(ids):
        inside = (ids[:, None] >= starts[None, :]) & (ids[:, None] < ends[None, :])
        return inside.astype(jnp.float32)

    member = member_of(row_ids)
    member_ph = member_of(mine)
    density_sq = jnp.sum(jnp.square(density_factor.astype(jnp.float32)), axis=1)
    ph_sq = jnp.sum(jnp.square(ph_factor.astype(jnp.float32)), axis=1)
    offset = row_index * block - col_index * width
    holds = (offset >= 0) & (offset < width)
    square = lax.dynamic_slice_in_dim(
        multiplier_g, jnp.clip(offset, 0, width - block), block, axis=1
    )
    keep = (index[:, None] == index[None, :]) & holds
    mult_diag = jnp.sum(jnp.where(keep, square.astype(jnp.float32), 0.0), axis=1)
    sums = lax.psum(
        jnp.stack(
            [
                jnp.sum(member * density_sq[:, None], axis=0),
                jnp.sum(member_ph * (mult_diag - penalty * ph_sq)[:, None], axis=0),
            ]
        ),
        both,
    )
    shift_means = 2.0 * sums[0] / lengths
    scale_means = 2.0 * (sums[1] + penalty * sums[0]) / lengths
    shift_rows = jnp.sum(member_ph * shift_means[None, :], axis=1)
    scale_rows = jnp.sum(member * scale_means[None, :], axis=1)

    pair_own = lax.all_gather(pair_local, "col", axis=0)
    ph_own = lax.all_gather(ph_local, "col", axis=0)
    offsets = offset.reshape(1)
    pair_part = apply_weight(
        pair_kernel, "pair", offsets, pair_own, pair_cols, multiplier_q, hamiltonian, True
    )
    pair_grad = lax.psum_scatter(pair_part, "col", scatter_dimension=0, tiled=False)
    ph_part = apply_weight(
        ph_kernel, "ph", offsets, ph_own, ph_cols, multiplier_g, shift_rows[:, None], False
    )
    ph_grad = lax.psum_scatter(ph_part, "col", scatter_dimension=0, tiled=False)

    back = select(take_hot, ph_grad[:, :rank_part], 0)
    back = lax.all_to_all(back, "row", split_axis=0, concat_axis=0, tiled=True)
    returned = select(send_hot, back, 1)
    grad_density = (
        2.0 * pair_grad[:, :rank_part]
        + 2.0 * scale_rows[:, None] * density_factor.astype(jnp.float32)
        + 2.0 * returned
    )
    grad_hole = 2.0 * pair_grad[:, rank_part:]
    grad_ph = 2.0 * ph_grad[:, rank_part:]
    return (grad_density, grad_hole, grad_ph)


def solution(mesh):
    return jax.shard_map(
        local,
        mesh=mesh,
        in_specs=(
            P("row", "col"),
            P("row", "col"),
            P("row", "col"),
            P("row", "col"),
            P("row", "col"),
            P("row", "col"),
            P(),
            P(),
        ),
        out_specs=(P("row", "col"), P("row", "col"), P("row", "col")),
        check_vma=False,
    )
```

time: 452 us -> 258 us (0.57)
  local copies, waits for them, and re-layouts: 131 us -> 24.1 us
  blocking collectives: 155 us -> 118 us
  waiting for transfers between devices: 74.7 us -> 46.9 us
  matrix products: 28.6 us -> 7.23 us
  Pallas kernels: 0 us -> 18.1 us
  other arithmetic: 22.9 us -> 12.8 us
  starting transfers between devices: 23.9 us -> 15.5 us
    gather x9 -> x0, local copies, waits for them, and re-layouts: 79.6 us -> none  [the longest x1 34.3 us: local(): shifted_ph = jnp.take(shifted, ph_perm)]
    all_gather x5 -> x2, blocking collectives: 86.9 us -> 21.2 us  [the longest x1 10.7 us: local(): ph_own = lax.all_gather(ph_local, 'col', axis=0)]
    all_gather x2, waiting for transfers between devices: 57.7 us -> 8.61 us  [whole_cols(): whole = lax.all_gather(placed, 'row', axis=0, tiled=True)]
    reduce_scatter x2, waiting for transfers between devices: 0.04 us -> 31.4 us  [the longest x1 20.1 us: local(): lax.psum_scatter(pair_part, 'col', scatter_dimension=0, tiled=False)]
    psum x1, blocking collectives: 67.9 us -> 97.1 us  [local(): lax.psum(jnp.stack([jnp.sum(member * density_sq[:, None], axis=0), jnp.su...]
    scatter x1 -> x0, local copies, waits for them, and re-layouts: 23 us -> none  [local(): weight_pair = jnp.zeros_like(weight_diag).at[ph_perm].set(weight_diag)]
    dot_general x3 -> x4, matrix products: 28.6 us -> 7.23 us  [select(): lax.dot_general(one_hot.astype(values.dtype), values, (((left_axis,), (0,...]
    pallas_call x0 -> x2, Pallas kernels: none -> 18.1 us  [apply_weight(): pl.pallas_call(kernel, name=name, out_shape=jax.ShapeDtypeStruct((parts,...]
  transfers between devices with their start and end apart: 8 -> 8, of which waited for: 3 -> 4; matrix products, arithmetic and copies ran while one was open for 36% -> 10% of each run, Pallas kernels for 0% -> 7%
where the time goes in v1:
time: 258 us; the launch traced here: 257 us
  blocking collectives  118 us (46%)
  waiting for transfers between devices  46.9 us (18%)
  local copies, waits for them, and re-layouts  24.1 us (9%)
  Pallas kernels  18.1 us (7%)
  starting transfers between devices  15.5 us (6%)
  between operations  13.9 us (5%)
  other arithmetic  12.8 us (5%)
  matrix products  7.23 us (3%)
    psum x1, blocking collectives, local(): lax.psum(jnp.stack([jnp.sum(member * density_sq[:, None], axis=0), jnp.su...  97.1 us
    reduce_scatter x1, waiting for transfers between devices, local(): lax.psum_scatter(pair_part, 'col', scatter_dimension=0, tiled=False)  20.1 us
    pallas_call x2, Pallas kernels, apply_weight(): pl.pallas_call(kernel, name=name, out_shape=jax.ShapeDtypeStruct((parts,...  18.1 us
    unnamed x18, local copies, waits for them, and re-layouts  13.1 us
    reduce_scatter x1, waiting for transfers between devices, local(): ph_grad = lax.psum_scatter(ph_part, 'col', scatter_dimension=0, tiled=False)  11.3 us
    all_gather x1, blocking collectives, local(): ph_own = lax.all_gather(ph_local, 'col', axis=0)  10.7 us
    all_gather x1, blocking collectives, local(): pair_own = lax.all_gather(pair_local, 'col', axis=0)  10.5 us
    all_gather x1, local copies, waits for them, and re-layouts, whole_cols(): whole = lax.all_gather(placed, 'row', axis=0, tiled=True)  9.03 us
  transfers between devices with their start and end apart: 8, of which 4 were waited for; matrix products, arithmetic and copies ran while one was open for 10% of the time, Pallas kernels for 7%

profile of v1, /device:TPU:0, one launch (start us, length us, event | category | flops | bytes accessed | tf_op | source)
XLA Modules:
  0.0 256.8 jit_solution(1267810612023310110)
XLA Ops:
  7.2 2.1 select_reduce_fusion
  9.3 0.3 convert_reduce_fusion.1
  9.6 2.0 convolution_convert_fusion.1
  11.7 7.4 %all-to-all-start = ((bf16[16,24,256]{2,1,0:T(8,128)(2,1)}), bf16[16,24,256]{2,1,0:T(8,128)(2,1)S(1)}, u32[]{:S(2)}, u32[]{:S(2)}) async-start(bf16[16,24,256]{2,1,0:T(8,128)(2,1)} %bitcast.7), calls=%async_computation.1 | async-start | bytes 393216 | tf_op jit(solution)/shard_map/all_to_all | solution.py:156
  19.1 0.0 all-gather.7.cloned.1.call-start
  19.1 0.8 add_select_fusion
  19.9 1.1 copy.18
  21.0 0.2 convert_reduce_fusion
  21.2 6.8 %all-to-all-done = bf16[16,24,256]{2,1,0:T(8,128)(2,1)S(1)} async-done(((bf16[16,24,256]{2,1,0:T(8,128)(2,1)}), bf16[16,24,256]{2,1,0:T(8,128)(2,1)S(1)}, u32[]{:S(2)}, u32[]{:S(2)}) %all-to-all-start) | async-done | bytes 196640 | tf_op jit(solution)/shard_map/all_to_all | solution.py:156
  28.0 0.4 convolution_convert_fusion
  28.5 0.7 collective-permute-start.1
  29.2 0.0 collective-permute-done.1
  29.2 0.0 copy-start.7
  29.2 0.7 copy-done.7
  29.9 0.0 all-gather.7.cloned.1.call-update
  30.0 0.0 all-gather.5.cloned.1.call-start
  30.0 1.6 constant_dynamic-update-slice_fusion.1
  31.6 1.6 constant_dynamic-update-slice_fusion
  33.2 1.6 collective-permute-start
  34.9 0.0 collective-permute-done
  34.9 0.0 copy-start.6
  34.9 0.7 copy-done.6
  35.6 0.0 all-gather.5.cloned.1.call-update
  35.7 0.0 reduce-scatter.5.cloned.1.call-start
  35.7 0.8 select_reduce_fusion.6
  36.5 0.7 sub.24
  37.2 1.2 select_reduce_fusion.1
  38.4 1.1 multiply_reduce_fusion
  39.4 1.1 fusion.4
  40.5 0.2 select_reduce_fusion.5
  40.7 97.1 %psum.7 = f32[2,48]{1,0:T(2,128)S(1)} all-reduce(f32[2,48]{1,0:T(2,128)S(1)} %pad_maximum_fusion.1), channel_id=1, replica_groups=mesh['row'=16,'col'=2] {'row','col'}, use_global_device_ids=true, to_apply=%region_7.8 | all-reduce | flops 96 | bytes 768 | tf_op jit(solution)/shard_map/psum | solution.py:182
  137.8 0.7 bitcast_divide_fusion
  138.5 0.1 select_reduce_fusion.3
  138.6 0.1 broadcast_in_dim.35.shift_ref
  138.7 10.7 %all-gather.1 = bf16[768,512]{0,1:T(8,128)(2,1)S(1)} all-gather(bf16[384,512]{0,1:T(8,128)(2,1)S(1)} %pad_maximum_fusion), channel_id=3, replica_groups=mesh['row'=16,'col'=2] {'col'}, dimensions={0}, use_global_device_ids=true | all-gather | bytes 1179648 | tf_op jit(solution)/shard_map/all_gather | solution.py:197
  149.4 0.3 copy.19
  149.7 0.0 copy-start.1
  149.7 0.0 all-gather.7.cloned.1.call-done
  149.7 9.0 %copy.20 = bf16[6144,512]{1,0:T(8,128)(2,1)} copy(bf16[6144,512]{0,1:T(8,128)(2,1)} %all-gather.7.cloned.1.call-done) | data formatting | bytes 12582912 | tf_op jit(solution)/shard_map/all_gather | solution.py:133
  158.8 0.0 copy-done.1
  158.8 0.0 copy-start
  158.8 2.8 %copy-done = bf16[6144,512]{1,0:T(8,128)(2,1)S(1)} copy-done((bf16[6144,512]{1,0:T(8,128)(2,1)S(1)}, bf16[6144,512]{1,0:T(8,128)(2,1)}, u32[]{:S(2)}) %copy-start) | copy-done | bytes 6291480
  161.5 8.4 %ph.1 = f32[2,384,512]{2,1,0:T(8,128)} custom-call(s32[1]{0:T(128)} %bitcast.offset_ref, bf16[2,384,512]{2,1,0:T(8,128)(2,1)S(1)} %bitcast.21, bf16[2,3072,512]{2,1,0:T(8,128)(2,1)S(1)} %bitcast.20, bf16[384,3072]{1,0:T(8,128)(2,1)S(1)} %copy-done.1, f32[384,1]{1,0:T(8,128)S(1)} %broadcast_in_dim.35.shift_ref), custom_call_target="tpu_custom_call" | custom-call | flops 4831838208 | bytes 11010048 | tf_op jit(solution)/shard_map/ph/pallas_call | solution.py:65
  169.9 0.0 reduce-scatter.5.cloned.1.call-update
  169.9 0.0 reduce-scatter.3.cloned.1.call-start
  170.0 10.5 %all-gather = bf16[768,512]{1,0:T(8,128)(2,1)S(1)} all-gather(bf16[384,512]{1,0:T(8,128)(2,1)} %constant_dynamic-update-slice_fusion), channel_id=2, replica_groups=mesh['row'=16,'col'=2] {'col'}, dimensions={0}, use_global_device_ids=true | all-gather | bytes 1179648 | tf_op jit(solution)/shard_map/all_gather | solution.py:196
  180.4 8.6 %all-gather.5.cloned.1.call-done = bf16[6144,512]{1,0:T(8,128)(2,1)} async-done(((bf16[384,512]{1,0:T(8,128)(2,1)}), bf16[6144,512]{1,0:T(8,128)(2,1)}) %all-gather.5.cloned.1.call-update) | async-done | bytes 6291472 | tf_op jit(solution)/shard_map/all_gather | solution.py:133
  189.0 0.0 copy-start.2
  189.0 2.8 %copy-done.2 = bf16[6144,512]{1,0:T(8,128)(2,1)S(1)} copy-done((bf16[6144,512]{1,0:T(8,128)(2,1)S(1)}, bf16[6144,512]{1,0:T(8,128)(2,1)}, u32[]{:S(2)}) %copy-start.2) | copy-done | bytes 6291480
  191.8 0.0 copy-start.3
  191.8 1.7 copy-done.3
  193.5 1.7 copy-done.4
  195.1 0.0 copy-start.5
  195.2 9.7 %pair.1 = f32[2,384,512]{2,1,0:T(8,128)} custom-call(s32[1]{0:T(128)} %bitcast.offset_ref, bf16[2,384,512]{2,1,0:T(8,128)(2,1)S(1)} %bitcast.22, bf16[2,3072,512]{2,1,0:T(8,128)(2,1)S(1)} %bitcast.23, bf16[384,3072]{1,0:T(8,128)(2,1)S(1)} %copy-done.3, bf16[384,3072]{1,0:T(8,128)(2,1)S(1)} %copy-done.4), custom_call_target="tpu_custom_call" | custom-call | flops 6039797760 | bytes 11010048 | tf_op jit(solution)/shard_map/pair/pallas_call | solution.py:65
  204.9 0.0 reduce-scatter.3.cloned.1.call-update
  204.9 11.3 %reduce-scatter.5.cloned.1.call-done = f32[1,384,512]{2,1,0:T(8,128)} async-done(((f32[2,384,512]{2,1,0:T(8,128)}), f32[1,384,512]{2,1,0:T(8,128)}) %reduce-scatter.5.cloned.1.call-update) | async-done | bytes 786448 | tf_op jit(solution)/shard_map/reduce_scatter | solution.py:206
  216.2 2.5 fusion.1
  218.7 5.6 %all-to-all-start.1 = ((f32[16,24,256]{2,1,0:T(8,128)}), f32[16,24,256]{2,1,0:T(8,128)S(1)}, u32[]{:S(2)}, u32[]{:S(2)}) async-start(f32[16,24,256]{2,1,0:T(8,128)} %bitcast.13), calls=%async_computation.3 | async-start | bytes 786432 | tf_op jit(solution)/shard_map/all_to_all | solution.py:209
  224.3 20.1 %reduce-scatter.3.cloned.1.call-done = f32[1,384,512]{2,1,0:T(8,128)} async-done(((f32[2,384,512]{2,1,0:T(8,128)}), f32[1,384,512]{2,1,0:T(8,128)}) %reduce-scatter.3.cloned.1.call-update) | async-done | bytes 786448 | tf_op jit(solution)/shard_map/reduce_scatter | solution.py:202
  244.4 1.8 slice_multiply_fusion.1
  246.2 1.8 slice_multiply_fusion
  248.0 0.0 all-to-all-done.1
  248.0 0.0 copy-done.5
  248.0 2.3 fusion
  (9 shorter events, 0.1 us)
Async XLA Ops:
  11.7 16.4 %all-to-all-start = ((bf16[16,24,256]{2,1,0:T(8,128)(2,1)}), bf16[16,24,256]{2,1,0:T(8,128)(2,1)S(1)}, u32[]{:S(2)}, u32[]{:S(2)}) async-start(bf16[16,24,256]{2,1,0:T(8,128)(2,1)} %bitcast.7), calls=%async_computation.1 | async-start | bytes 393216 | tf_op jit(solution)/shard_map/all_to_all | solution.py:156
  19.1 130.6 %all-gather.7.cloned.1.call-start = ((), (), s32[]{:S(2)}) async-start(), calls=%async_computation.6 | async-start | bytes 6684672 | tf_op jit(solution)/shard_map/all_gather | solution.py:133
  28.5 0.7 collective-permute-start.1
  29.2 0.7 copy-start.7
  30.0 159.1 %all-gather.5.cloned.1.call-start = ((), (), s32[]{:S(2)}) async-start(), calls=%async_computation.4 | async-start | bytes 6684672 | tf_op jit(solution)/shard_map/all_gather | solution.py:133
  33.2 1.6 collective-permute-start
  34.9 0.7 copy-start.6
  35.7 180.5 %reduce-scatter.5.cloned.1.call-start = ((), (), s32[]{:S(2)}) async-start(), calls=%async_computation.7 | async-start | bytes 2359296 | tf_op jit(solution)/shard_map/reduce_scatter | solution.py:206
  149.7 9.1 %copy-start.1 = (bf16[384,3072]{1,0:T(8,128)(2,1)S(1)}, bf16[384,3072]{1,0:T(8,128)(2,1)}, u32[]{:S(2)}) copy-start(bf16[384,3072]{1,0:T(8,128)(2,1)} %mult_ref.3) | copy-start | bytes 7077892
  158.8 2.8 %copy-start = (bf16[6144,512]{1,0:T(8,128)(2,1)S(1)}, bf16[6144,512]{1,0:T(8,128)(2,1)}, u32[]{:S(2)}) copy-start(bf16[6144,512]{1,0:T(8,128)(2,1)} %copy.20) | copy-start | bytes 18874372
  169.9 74.5 %reduce-scatter.3.cloned.1.call-start = ((), (), s32[]{:S(2)}) async-start(), calls=%async_computation.5 | async-start | bytes 2359296 | tf_op jit(solution)/shard_map/reduce_scatter | solution.py:202
  189.0 2.8 %copy-start.2 = (bf16[6144,512]{1,0:T(8,128)(2,1)S(1)}, bf16[6144,512]{1,0:T(8,128)(2,1)}, u32[]{:S(2)}) copy-start(bf16[6144,512]{1,0:T(8,128)(2,1)} %all-gather.5.cloned.1.call-done) | copy-start | bytes 18874372
  191.8 1.7 copy-start.3
  193.5 1.7 copy-start.4
  195.1 52.8 %copy-start.5 = (bf16[384,256]{1,0:T(8,128)(2,1)S(1)}, bf16[384,256]{1,0:T(8,128)(2,1)}, u32[]{:S(2)}) copy-start(bf16[384,256]{1,0:T(8,128)(2,1)} %param.8) | copy-start | bytes 589828
  218.7 29.3 %all-to-all-start.1 = ((f32[16,24,256]{2,1,0:T(8,128)}), f32[16,24,256]{2,1,0:T(8,128)S(1)}, u32[]{:S(2)}, u32[]{:S(2)}) async-start(f32[16,24,256]{2,1,0:T(8,128)} %bitcast.13), calls=%async_computation.3 | async-start | bytes 786432 | tf_op jit(solution)/shard_map/all_to_all | solution.py:209
Sparse Core Ops, SparseCore 0:
  30.1 96.3 all-gather.6
  129.4 59.6 all-gather.4
  191.3 24.8 reduce-scatter.4
  218.3 26.1 reduce-scatter.2

commit v2 on v1

--- a/solution.py
+++ b/solution.py
@@ -1,3 +1,5 @@
+import functools
+
 import jax
 import jax.numpy as jnp
 from jax import lax
@@ -88,6 +90,201 @@
     )(offset, own, cols, mult, extra)
 
 
+MESH = pl.DeviceIdType.MESH
+
+
+def spread_kernel(
+    groups,
+    col_groups,
+    pair_ref,
+    ph_ref,
+    pair_cols,
+    ph_cols,
+    pair_own,
+    ph_own,
+    place_send,
+    place_recv,
+    own_send,
+    own_recv,
+    ring_send,
+    ring_recv,
+    mate_send,
+    mate_recv,
+    here_sem,
+):
+    row = lax.axis_index("row")
+    col = lax.axis_index("col")
+    per = groups // col_groups
+    chips = groups // 2
+    half = chips // 2
+    block = pair_ref.shape[0]
+    core = row % 2
+    chip = row // 2
+    pos = jnp.where(chip % 2 == 0, chip // 2, chips - 1 - chip // 2)
+
+    def row_at(place, which):
+        place = (place + chips) % chips
+        return jnp.where(place < half, 2 * place, 2 * (chips - 1 - place) + 1) * 2 + which
+
+    ring_to = [(row_at(pos + 1, core), col), (row_at(pos - 1, core), col)]
+    mate = (row + 1 - 2 * core, col)
+    home = row // per
+    moved = col != home
+    partner = (col * per + row % per, home)
+    peers = [(row, (col + d) % col_groups) for d in range(1, col_groups)]
+
+    barrier = pltpu.get_barrier_semaphore()
+    for device in ring_to + [mate] + peers:
+        pl.semaphore_signal(barrier, inc=1, device_id=device, device_id_type=MESH)
+
+    @pl.when(moved)
+    def _():
+        pl.semaphore_signal(barrier, inc=1, device_id=partner, device_id_type=MESH)
+
+    pl.semaphore_wait(barrier, jnp.where(moved, 4 + len(peers), 3 + len(peers)))
+
+    locals_ = [pair_ref, ph_ref]
+    cols_ = [pair_cols, ph_cols]
+    owns_ = [pair_own, ph_own]
+
+    def placing(a):
+        return pltpu.make_async_remote_copy(
+            src_ref=locals_[a],
+            dst_ref=cols_[a].at[partner[0]],
+            send_sem=place_send.at[a],
+            recv_sem=place_recv.at[a],
+            device_id=partner,
+            device_id_type=MESH,
+        )
+
+    def staying(a):
+        return pltpu.make_async_copy(locals_[a], cols_[a].at[row], here_sem.at[a, 0])
+
+    def keeping(a):
+        return pltpu.make_async_copy(locals_[a], owns_[a].at[col], here_sem.at[a, 1])
+
+    def owning(a, d, origin):
+        return pltpu.make_async_remote_copy(
+            src_ref=locals_[a],
+            dst_ref=owns_[a].at[origin],
+            send_sem=own_send.at[a, d - 1],
+            recv_sem=own_recv.at[a, d - 1],
+            device_id=peers[d - 1],
+            device_id_type=MESH,
+        )
+
+    def piece(a, slot, way, step):
+        if step == half:
+            return cols_[a].at[slot, pl.ds(way * (block // 2), block // 2)]
+        return cols_[a].at[slot]
+
+    def ring(a, way, step, travelled):
+        sign = -1 if way == 0 else 1
+        ref = piece(a, row_at(pos + sign * travelled, core), way, step)
+        return pltpu.make_async_remote_copy(
+            src_ref=ref,
+            dst_ref=ref,
+            send_sem=ring_send.at[a, way, step - 1],
+            recv_sem=ring_recv.at[a, way, step - 1],
+            device_id=ring_to[way],
+            device_id_type=MESH,
+        )
+
+    def mating(a, way, step, which):
+        sign = -1 if way == 0 else 1
+        ref = piece(a, row_at(pos + sign * step, which), way, step)
+        return pltpu.make_async_remote_copy(
+            src_ref=ref,
+            dst_ref=ref,
+            send_sem=mate_send.at[a, way, step],
+            recv_sem=mate_recv.at[a, way, step],
+            device_id=mate,
+            device_id_type=MESH,
+        )
+
+    for a in range(2):
+
+        @pl.when(moved)
+        def _():
+            placing(a).start()
+
+        @pl.when(jnp.logical_not(moved))
+        def _():
+            staying(a).start()
+
+        keeping(a).start()
+
+    for a in range(2):
+
+        @pl.when(moved)
+        def _():
+            placing(a).wait_recv()
+
+        @pl.when(jnp.logical_not(moved))
+        def _():
+            staying(a).wait()
+
+        for way in range(2):
+            ring(a, way, 1, 0).start()
+        mating(a, 0, 0, core).start()
+
+    for a in range(2):
+        for d in range(1, col_groups):
+            owning(a, d, col).start()
+
+    for step in range(1, half + 1):
+        for a in range(2):
+            for way in range(2):
+                ring(a, way, step, step).wait_recv()
+                if step < half:
+                    ring(a, way, step + 1, step).start()
+                mating(a, way, step, core).start()
+
+    for a in range(2):
+        mating(a, 0, 0, 1 - core).wait_recv()
+        mating(a, 0, 0, core).wait_send()
+        for step in range(1, half + 1):
+            for way in range(2):
+                mating(a, way, step, 1 - core).wait_recv()
+                mating(a, way, step, core).wait_send()
+                ring(a, way, step, step - 1).wait_send()
+        for d in range(1, col_groups):
+            owning(a, d, (col + col_groups - d) % col_groups).wait_recv()
+            owning(a, d, col).wait_send()
+        keeping(a).wait()
+
+        @pl.when(moved)
+        def _():
+            placing(a).wait_send()
+
+
+def spread(groups, col_groups, pair_local, ph_local):
+    block, depth = pair_local.shape
+    half = groups // 4
+    dma = pltpu.SemaphoreType.DMA
+    cols = jax.ShapeDtypeStruct((groups, block, depth), pair_local.dtype)
+    own = jax.ShapeDtypeStruct((col_groups, block, depth), pair_local.dtype)
+    return pl.pallas_call(
+        functools.partial(spread_kernel, groups, col_groups),
+        name="spread",
+        out_shape=(cols, cols, own, own),
+        in_specs=[pl.BlockSpec(memory_space=pltpu.VMEM)] * 2,
+        out_specs=(pl.BlockSpec(memory_space=pl.ANY),) * 4,
+        scratch_shapes=[
+            dma((2,)),
+            dma((2,)),
+            dma((2, max(col_groups - 1, 1))),
+            dma((2, max(col_groups - 1, 1))),
+            dma((2, 2, half)),
+            dma((2, 2, half)),
+            dma((2, 2, half + 1)),
+            dma((2, 2, half + 1)),
+            dma((2, 2)),
+        ],
+        compiler_params=pltpu.CompilerParams(collective_id=0, has_side_effects=True),
+    )(pair_local, ph_local)
+
+
 def select(one_hot, values, left_axis):
     if values.dtype == jnp.float32:
         precision = lax.Precision.HIGHEST
@@ -119,22 +316,8 @@
     block, rank_part = density_factor.shape
     width = multiplier_q.shape[1]
     sends = block // groups
-    per = groups // col_groups
     both = ("row", "col")
-
-    placing = [
-        (r * col_groups + c, (c * per + r % per) * col_groups + r // per)
-        for r in range(groups)
-        for c in range(col_groups)
-    ]
-
-    def whole_cols(piece):
-        placed = lax.ppermute(piece, both, placing)
-        whole = lax.all_gather(placed, "row", axis=0, tiled=True)
-        return whole.reshape(col_groups, width, 2 * rank_part)
-
     pair_local = jnp.concatenate([density_factor, hole_factor], axis=1)
-    pair_cols = whole_cols(pair_local)
 
     index = jnp.arange(block, dtype=jnp.int32)
     row_ids = row_index * block + index
@@ -156,7 +339,6 @@
     incoming = lax.all_to_all(outgoing, "row", split_axis=0, concat_axis=0, tiled=True)
     density_ph = select(take_hot, incoming, 1)
     ph_local = jnp.concatenate([density_ph, ph_factor], axis=1)
-    ph_cols = whole_cols(ph_local)
 
     lengths = block_lengths.astype(jnp.float32)
     count = block_lengths.shape[0]
@@ -193,8 +375,9 @@
     shift_rows = jnp.sum(member_ph * shift_means[None, :], axis=1)
     scale_rows = jnp.sum(member * scale_means[None, :], axis=1)
 
-    pair_own = lax.all_gather(pair_local, "col", axis=0)
-    ph_own = lax.all_gather(ph_local, "col", axis=0)
+    pair_cols, ph_cols, pair_own, ph_own = spread(groups, col_groups, pair_local, ph_local)
+    pair_cols = pair_cols.reshape(col_groups, width, 2 * rank_part)
+    ph_cols = ph_cols.reshape(col_groups, width, 2 * rank_part)
     offsets = offset.reshape(1)
     pair_part = apply_weight(
         pair_kernel, "pair", offsets, pair_own, pair_cols, multiplier_q, hamiltonian, True

time: 258 us -> 249 us (0.965)
  Pallas kernels: 18.1 us -> 115 us
  blocking collectives: 118 us -> 40.7 us
  waiting for transfers between devices: 46.9 us -> 31.8 us
  local copies, waits for them, and re-layouts: 24.1 us -> 10.1 us
  other arithmetic: 12.8 us -> 16.3 us
    pallas_call x0 -> x1, Pallas kernels: none -> 96.9 us  [spread(): pl.pallas_call(functools.partial(spread_kernel, groups, col_groups), name...]
    psum x1, blocking collectives: 97.1 us -> 40.7 us  [local(): lax.psum(jnp.stack([jnp.sum(member * density_sq[:, None], axis=0), jnp.su...]
    all_gather x2 -> x0, blocking collectives: 21.2 us -> none  [the longest x1 10.7 us: local(): ph_own = lax.all_gather(ph_local, 'col', axis=0)]
    all_gather x2 -> x0, local copies, waits for them, and re-layouts: 9.31 us -> none  [the longest x1 9.03 us: whole_cols(): whole = lax.all_gather(placed, 'row', axis=0, tiled=True)]
    all_gather x2 -> x0, waiting for transfers between devices: 8.61 us -> none  [whole_cols(): whole = lax.all_gather(placed, 'row', axis=0, tiled=True)]
    all_to_all x1, waiting for transfers between devices: 6.79 us -> 0.01 us  [local(): lax.all_to_all(outgoing, 'row', split_axis=0, concat_axis=0, tiled=True)]
    unnamed x18 -> x16, local copies, waits for them, and re-layouts: 13.1 us -> 10 us
  transfers between devices with their start and end apart: 8 -> 4, of which waited for: 4 -> 2; matrix products, arithmetic and copies ran while one was open for 10% -> 6% of each run, Pallas kernels for 7% -> 4%
where the time goes in v2:
time: 249 us; the launch traced here: 248 us
  Pallas kernels  115 us (46%)
  blocking collectives  40.7 us (16%)
  waiting for transfers between devices  31.8 us (13%)
  other arithmetic  16.3 us (7%)
  between operations  14.2 us (6%)
  starting transfers between devices  13.1 us (5%)
  local copies, waits for them, and re-layouts  10.1 us (4%)
  matrix products  7.14 us (3%)
    pallas_call x1, Pallas kernels, spread(): pl.pallas_call(functools.partial(spread_kernel, groups, col_groups), name...  96.9 us
    psum x1, blocking collectives, local(): lax.psum(jnp.stack([jnp.sum(member * density_sq[:, None], axis=0), jnp.su...  40.7 us
    reduce_scatter x1, waiting for transfers between devices, local(): lax.psum_scatter(pair_part, 'col', scatter_dimension=0, tiled=False)  18.5 us
    pallas_call x2, Pallas kernels, apply_weight(): pl.pallas_call(kernel, name=name, out_shape=jax.ShapeDtypeStruct((parts,...  18.1 us
    reduce_scatter x1, waiting for transfers between devices, local(): ph_grad = lax.psum_scatter(ph_part, 'col', scatter_dimension=0, tiled=False)  13.3 us
    unnamed x16, local copies, waits for them, and re-layouts  10 us
    all_to_all x1, starting transfers between devices, local(): lax.all_to_all(outgoing, 'row', split_axis=0, concat_axis=0, tiled=True)  7.38 us
    dot_general x4, matrix products, select(): lax.dot_general(one_hot.astype(values.dtype), values, (((left_axis,), (0,...  7.14 us
  transfers between devices with their start and end apart: 4, of which 2 were waited for; matrix products, arithmetic and copies ran while one was open for 6% of the time, Pallas kernels for 4%

profile of v2, /device:TPU:0, one launch (start us, length us, event | category | flops | bytes accessed | tf_op | source)
XLA Modules:
  0.0 248.3 jit_solution(7259494562836915910)
XLA Ops:
  7.2 0.8 add_select_fusion.1
  8.0 2.1 select_reduce_fusion
  10.1 0.3 convert_reduce_fusion
  10.4 2.0 convolution_convert_fusion.1
  12.4 7.4 %all-to-all-start = ((bf16[16,24,256]{2,1,0:T(8,128)(2,1)}), bf16[16,24,256]{2,1,0:T(8,128)(2,1)S(1)}, u32[]{:S(2)}, u32[]{:S(2)}) async-start(bf16[16,24,256]{2,1,0:T(8,128)(2,1)} %bitcast.1), calls=%async_computation | async-start | bytes 393216 | tf_op jit(solution)/shard_map/all_to_all | solution.py:339
  19.8 0.0 reduce-scatter.5.cloned.1.call-start
  19.9 1.1 fusion.4
  21.0 1.8 pad_maximum_fusion.pair_ref
  22.8 1.1 multiply_reduce_fusion
  23.8 0.8 select_reduce_fusion.6
  24.6 0.7 sub.26
  25.3 1.2 select_reduce_fusion.1
  26.5 0.2 select_reduce_fusion.5
  26.7 40.7 %psum.7 = f32[2,48]{1,0:T(2,128)S(1)} all-reduce(f32[2,48]{1,0:T(2,128)S(1)} %pad_maximum_fusion.2), channel_id=1, replica_groups=mesh['row'=16,'col'=2] {'row','col'}, use_global_device_ids=true, to_apply=%region_10.11 | all-reduce | flops 96 | bytes 768 | tf_op jit(solution)/shard_map/psum | solution.py:364
  67.3 0.7 bitcast_divide_fusion
  68.0 0.1 select_reduce_fusion.3
  68.1 0.1 broadcast_in_dim.35.shift_ref
  68.2 0.2 convert_reduce_fusion.1
  68.5 0.0 all-to-all-done
  68.5 0.3 convolution_convert_fusion
  68.8 1.7 pad_maximum_fusion.1.ph_ref
  70.5 96.9 %spread.1 = (bf16[16,384,512]{2,1,0:T(8,128)(2,1)}, bf16[16,384,512]{2,1,0:T(8,128)(2,1)}, bf16[2,384,512]{2,1,0:T(8,128)(2,1)}, bf16[2,384,512]{2,1,0:T(8,128)(2,1)}) custom-call(bf16[384,512]{1,0:T(8,128)(2,1)} %pad_maximum_fusion.pair_ref, bf16[384,512]{1,0:T(8,128)(2,1)} %pad_maximum_fusion.1.ph_ref), custom_call_target="tpu_custom_call" | custom-call | tf_op jit(solution)/shard_map/spread/pallas_call | solution.py:267
  167.4 0.0 copy-start
  167.4 1.7 copy-done
  169.1 0.0 copy-start.2
  169.1 2.8 %copy-done.2 = bf16[16,384,512]{2,1,0:T(8,128)(2,1)S(1)} copy-done((bf16[16,384,512]{2,1,0:T(8,128)(2,1)S(1)}, bf16[16,384,512]{2,1,0:T(8,128)(2,1)}, u32[]{:S(2)}) %copy-start.2) | copy-done | bytes 6291480
  171.9 0.0 copy-start.6
  171.9 1.1 copy-done.6
  173.0 0.0 copy-start.3
  173.0 0.0 copy-start.5
  173.0 8.4 %ph.1 = f32[2,384,512]{2,1,0:T(8,128)} custom-call(s32[1]{0:T(128)} %bitcast.offset_ref, bf16[2,384,512]{2,1,0:T(8,128)(2,1)S(1)} %copy-done.6, bf16[2,3072,512]{2,1,0:T(8,128)(2,1)S(1)} %bitcast.19, bf16[384,3072]{1,0:T(8,128)(2,1)S(1)} %copy-done, f32[384,1]{1,0:T(8,128)S(1)} %broadcast_in_dim.35.shift_ref), custom_call_target="tpu_custom_call" | custom-call | flops 4831838208 | bytes 11010048 | tf_op jit(solution)/shard_map/ph/pallas_call | solution.py:67
  181.4 0.0 reduce-scatter.5.cloned.1.call-update
  181.4 0.0 reduce-scatter.3.cloned.1.call-start
  181.4 0.0 copy-done.3
  181.4 0.0 copy-done.5
  181.5 0.0 copy-start.1
  181.5 2.8 %copy-done.1 = bf16[16,384,512]{2,1,0:T(8,128)(2,1)S(1)} copy-done((bf16[16,384,512]{2,1,0:T(8,128)(2,1)S(1)}, bf16[16,384,512]{2,1,0:T(8,128)(2,1)}, u32[]{:S(2)}) %copy-start.1) | copy-done | bytes 6291480
  184.2 0.0 copy-start.4
  184.2 1.7 copy-done.4
  185.9 0.0 copy-start.7
  185.9 9.7 %pair.1 = f32[2,384,512]{2,1,0:T(8,128)} custom-call(s32[1]{0:T(128)} %bitcast.offset_ref, bf16[2,384,512]{2,1,0:T(8,128)(2,1)S(1)} %copy-done.5, bf16[2,3072,512]{2,1,0:T(8,128)(2,1)S(1)} %bitcast.18, bf16[384,3072]{1,0:T(8,128)(2,1)S(1)} %copy-done.3, bf16[384,3072]{1,0:T(8,128)(2,1)S(1)} %copy-done.4), custom_call_target="tpu_custom_call" | custom-call | flops 6039797760 | bytes 11010048 | tf_op jit(solution)/shard_map/pair/pallas_call | solution.py:67
  195.6 0.0 reduce-scatter.3.cloned.1.call-update
  195.7 13.3 %reduce-scatter.5.cloned.1.call-done = f32[1,384,512]{2,1,0:T(8,128)} async-done(((f32[2,384,512]{2,1,0:T(8,128)}), f32[1,384,512]{2,1,0:T(8,128)}) %reduce-scatter.5.cloned.1.call-update) | async-done | bytes 786448 | tf_op jit(solution)/shard_map/reduce_scatter | solution.py:389
  209.0 2.5 %fusion.1 = f32[384,256]{1,0:T(8,128)} fusion(f32[384,512]{1,0:T(8,128)} %bitcast.21, s32[384]{0:T(512)S(1)} %multiply_add_fusion.1), kind=kOutput, calls=%fused_computation.10 | convolution fusion | flops 453132288 | bytes 787968 | tf_op jit(solution)/shard_map/dot_general | solution.py:293
  211.5 5.6 %all-to-all-start.1 = ((f32[16,24,256]{2,1,0:T(8,128)}), f32[16,24,256]{2,1,0:T(8,128)S(1)}, u32[]{:S(2)}, u32[]{:S(2)}) async-start(f32[16,24,256]{2,1,0:T(8,128)} %bitcast.11), calls=%async_computation.3 | async-start | bytes 786432 | tf_op jit(solution)/shard_map/all_to_all | solution.py:392
  217.1 1.8 slice_multiply_fusion
  218.9 18.5 %reduce-scatter.3.cloned.1.call-done = f32[1,384,512]{2,1,0:T(8,128)} async-done(((f32[2,384,512]{2,1,0:T(8,128)}), f32[1,384,512]{2,1,0:T(8,128)}) %reduce-scatter.3.cloned.1.call-update) | async-done | bytes 786448 | tf_op jit(solution)/shard_map/reduce_scatter | solution.py:385
  237.4 1.8 slice_multiply_fusion.1
  239.2 0.0 all-to-all-done.1
  239.2 0.0 copy-done.7
  239.2 2.3 fusion
  (6 shorter events, 0.1 us)
Async XLA Ops:
  12.4 56.0 %all-to-all-start = ((bf16[16,24,256]{2,1,0:T(8,128)(2,1)}), bf16[16,24,256]{2,1,0:T(8,128)(2,1)S(1)}, u32[]{:S(2)}, u32[]{:S(2)}) async-start(bf16[16,24,256]{2,1,0:T(8,128)(2,1)} %bitcast.1), calls=%async_computation | async-start | bytes 393216 | tf_op jit(solution)/shard_map/all_to_all | solution.py:339
  19.8 189.1 %reduce-scatter.5.cloned.1.call-start = ((), (), s32[]{:S(2)}) async-start(), calls=%async_computation.5 | async-start | bytes 2359296 | tf_op jit(solution)/shard_map/reduce_scatter | solution.py:389
  167.4 1.7 copy-start
  169.1 2.8 %copy-start.2 = (bf16[16,384,512]{2,1,0:T(8,128)(2,1)S(1)}, bf16[16,384,512]{2,1,0:T(8,128)(2,1)}, u32[]{:S(2)}) copy-start(bf16[16,384,512]{2,1,0:T(8,128)(2,1)} %get-tuple-element.10) | copy-start | bytes 18874372
  171.9 1.1 copy-start.6
  173.0 8.4 %copy-start.3 = (bf16[384,3072]{1,0:T(8,128)(2,1)S(1)}, bf16[384,3072]{1,0:T(8,128)(2,1)}, u32[]{:S(2)}) copy-start(bf16[384,3072]{1,0:T(8,128)(2,1)} %mult_ref.2) | copy-start | bytes 7077892
  173.0 8.4 %copy-start.5 = (bf16[2,384,512]{2,1,0:T(8,128)(2,1)S(1)}, bf16[2,384,512]{2,1,0:T(8,128)(2,1)}, u32[]{:S(2)}) copy-start(bf16[2,384,512]{2,1,0:T(8,128)(2,1)} %get-tuple-element.7.own_ref) | copy-start | bytes 2359300
  181.4 56.0 %reduce-scatter.3.cloned.1.call-start = ((), (), s32[]{:S(2)}) async-start(), calls=%async_computation.4 | async-start | bytes 2359296 | tf_op jit(solution)/shard_map/reduce_scatter | solution.py:385
  181.5 2.8 %copy-start.1 = (bf16[16,384,512]{2,1,0:T(8,128)(2,1)S(1)}, bf16[16,384,512]{2,1,0:T(8,128)(2,1)}, u32[]{:S(2)}) copy-start(bf16[16,384,512]{2,1,0:T(8,128)(2,1)} %get-tuple-element.8) | copy-start | bytes 18874372
  184.2 1.7 copy-start.4
  185.9 53.3 %copy-start.7 = (bf16[384,256]{1,0:T(8,128)(2,1)S(1)}, bf16[384,256]{1,0:T(8,128)(2,1)}, u32[]{:S(2)}) copy-start(bf16[384,256]{1,0:T(8,128)(2,1)} %param.8) | copy-start | bytes 589828
  211.5 27.7 %all-to-all-start.1 = ((f32[16,24,256]{2,1,0:T(8,128)}), f32[16,24,256]{2,1,0:T(8,128)S(1)}, u32[]{:S(2)}, u32[]{:S(2)}) async-start(f32[16,24,256]{2,1,0:T(8,128)} %bitcast.11), calls=%async_computation.3 | async-start | bytes 786432 | tf_op jit(solution)/shard_map/all_to_all | solution.py:392
Sparse Core Ops, SparseCore 0:
  181.5 27.4 reduce-scatter.4
  211.2 26.1 reduce-scatter.2

commit v3 on v2

--- a/solution.py
+++ b/solution.py
@@ -98,10 +98,12 @@
     col_groups,
     pair_ref,
     ph_ref,
+    stats_ref,
     pair_cols,
     ph_cols,
     pair_own,
     ph_own,
+    stats_all,
     place_send,
     place_recv,
     own_send,
@@ -111,6 +113,10 @@
     mate_send,
     mate_recv,
     here_sem,
+    stats_send,
+    stats_recv,
+    rows_send,
+    rows_recv,
 ):
     row = lax.axis_index("row")
     col = lax.axis_index("col")
@@ -133,15 +139,18 @@
     partner = (col * per + row % per, home)
     peers = [(row, (col + d) % col_groups) for d in range(1, col_groups)]
 
+    others = [(row + d) % groups for d in range(1, groups)]
+
     barrier = pltpu.get_barrier_semaphore()
-    for device in ring_to + [mate] + peers:
+    for device in [(other, col) for other in others] + peers:
         pl.semaphore_signal(barrier, inc=1, device_id=device, device_id_type=MESH)
 
     @pl.when(moved)
     def _():
         pl.semaphore_signal(barrier, inc=1, device_id=partner, device_id_type=MESH)
 
-    pl.semaphore_wait(barrier, jnp.where(moved, 4 + len(peers), 3 + len(peers)))
+    greeted = len(others) + len(peers)
+    pl.semaphore_wait(barrier, jnp.where(moved, greeted + 1, greeted))
 
     locals_ = [pair_ref, ph_ref]
     cols_ = [pair_cols, ph_cols]
@@ -202,6 +211,32 @@
             device_id_type=MESH,
         )
 
+    def stats_here():
+        return pltpu.make_async_copy(stats_ref, stats_all.at[row, col], here_sem.at[0, 2])
+
+    def stats_over(d, origin):
+        return pltpu.make_async_remote_copy(
+            src_ref=stats_ref,
+            dst_ref=stats_all.at[row, origin],
+            send_sem=stats_send.at[d - 1],
+            recv_sem=stats_recv.at[d - 1],
+            device_id=peers[d - 1],
+            device_id_type=MESH,
+        )
+
+    def stats_rows(d, origin):
+        return pltpu.make_async_remote_copy(
+            src_ref=stats_all.at[origin],
+            dst_ref=stats_all.at[origin],
+            send_sem=rows_send.at[d - 1],
+            recv_sem=rows_recv.at[d - 1],
+            device_id=(others[d - 1], col),
+            device_id_type=MESH,
+        )
+
+    stats_here().start()
+    for d in range(1, col_groups):
+        stats_over(d, col).start()
     for a in range(2):
 
         @pl.when(moved)
@@ -213,6 +248,12 @@
             staying(a).start()
 
         keeping(a).start()
+
+    stats_here().wait()
+    for d in range(1, col_groups):
+        stats_over(d, (col + col_groups - d) % col_groups).wait_recv()
+    for d in range(1, groups):
+        stats_rows(d, row).start()
 
     for a in range(2):
 
@@ -240,6 +281,11 @@
                     ring(a, way, step + 1, step).start()
                 mating(a, way, step, core).start()
 
+    for d in range(1, col_groups):
+        stats_over(d, col).wait_send()
+    for d in range(1, groups):
+        stats_rows(d, (row + groups - d) % groups).wait_recv()
+        stats_rows(d, row).wait_send()
     for a in range(2):
         mating(a, 0, 0, 1 - core).wait_recv()
         mating(a, 0, 0, core).wait_send()
@@ -258,7 +304,7 @@
             placing(a).wait_send()
 
 
-def spread(groups, col_groups, pair_local, ph_local):
+def spread(groups, col_groups, pair_local, ph_local, stats):
     block, depth = pair_local.shape
     half = groups // 4
     dma = pltpu.SemaphoreType.DMA
@@ -267,9 +313,15 @@
     return pl.pallas_call(
         functools.partial(spread_kernel, groups, col_groups),
         name="spread",
-        out_shape=(cols, cols, own, own),
-        in_specs=[pl.BlockSpec(memory_space=pltpu.VMEM)] * 2,
-        out_specs=(pl.BlockSpec(memory_space=pl.ANY),) * 4,
+        out_shape=(
+            cols,
+            cols,
+            own,
+            own,
+            jax.ShapeDtypeStruct((groups, col_groups) + stats.shape, stats.dtype),
+        ),
+        in_specs=[pl.BlockSpec(memory_space=pltpu.VMEM)] * 3,
+        out_specs=(pl.BlockSpec(memory_space=pl.ANY),) * 5,
         scratch_shapes=[
             dma((2,)),
             dma((2,)),
@@ -279,10 +331,14 @@
             dma((2, 2, half)),
             dma((2, 2, half + 1)),
             dma((2, 2, half + 1)),
-            dma((2, 2)),
+            dma((2, 3)),
+            dma((max(col_groups - 1, 1),)),
+            dma((max(col_groups - 1, 1),)),
+            dma((groups - 1,)),
+            dma((groups - 1,)),
         ],
         compiler_params=pltpu.CompilerParams(collective_id=0, has_side_effects=True),
-    )(pair_local, ph_local)
+    )(pair_local, ph_local, stats)
 
 
 def select(one_hot, values, left_axis):
@@ -316,7 +372,6 @@
     block, rank_part = density_factor.shape
     width = multiplier_q.shape[1]
     sends = block // groups
-    both = ("row", "col")
     pair_local = jnp.concatenate([density_factor, hole_factor], axis=1)
 
     index = jnp.arange(block, dtype=jnp.int32)
@@ -361,21 +416,22 @@
     )
     keep = (index[:, None] == index[None, :]) & holds
     mult_diag = jnp.sum(jnp.where(keep, square.astype(jnp.float32), 0.0), axis=1)
-    sums = lax.psum(
-        jnp.stack(
-            [
-                jnp.sum(member * density_sq[:, None], axis=0),
-                jnp.sum(member_ph * (mult_diag - penalty * ph_sq)[:, None], axis=0),
-            ]
-        ),
-        both,
-    )
+    sums = jnp.stack(
+        [
+            jnp.sum(member * density_sq[:, None], axis=0),
+            jnp.sum(member_ph * (mult_diag - penalty * ph_sq)[:, None], axis=0),
+        ]
+    )
+    stats = jnp.pad(sums, ((0, 6), (0, -count % 128)))
+    pair_cols, ph_cols, pair_own, ph_own, stats_all = spread(
+        groups, col_groups, pair_local, ph_local, stats
+    )
+    sums = jnp.sum(stats_all, axis=(0, 1))[:, :count]
     shift_means = 2.0 * sums[0] / lengths
     scale_means = 2.0 * (sums[1] + penalty * sums[0]) / lengths
     shift_rows = jnp.sum(member_ph * shift_means[None, :], axis=1)
     scale_rows = jnp.sum(member * scale_means[None, :], axis=1)
 
-    pair_cols, ph_cols, pair_own, ph_own = spread(groups, col_groups, pair_local, ph_local)
     pair_cols = pair_cols.reshape(col_groups, width, 2 * rank_part)
     ph_cols = ph_cols.reshape(col_groups, width, 2 * rank_part)
     offsets = offset.reshape(1)

time: 249 us -> 216 us (0.87)
  blocking collectives: 40.7 us -> 0 us
  Pallas kernels: 115 us -> 120 us
    psum x1 -> x0, blocking collectives: 40.7 us -> none  [local(): lax.psum(jnp.stack([jnp.sum(member * density_sq[:, None], axis=0), jnp.su...]
    pallas_call x1, Pallas kernels: 96.9 us -> 102 us  [spread(): pl.pallas_call(functools.partial(spread_kernel, groups, col_groups), name...]
  transfers between devices with their start and end apart: 4 -> 4, of which waited for: 2 -> 3; matrix products, arithmetic and copies ran while one was open for 6% -> 6% of each run, Pallas kernels for 4% -> 5%
where the time goes in v3:
time: 216 us; the launch traced here: 215 us
  Pallas kernels  120 us (56%)
  waiting for transfers between devices  32.8 us (15%)
  other arithmetic  17.8 us (8%)
  between operations  14.2 us (7%)
  starting transfers between devices  13.1 us (6%)
  local copies, waits for them, and re-layouts  10.1 us (5%)
  matrix products  7.13 us (3%)
    pallas_call x1, Pallas kernels, spread(): pl.pallas_call(functools.partial(spread_kernel, groups, col_groups), name...  102 us
    reduce_scatter x1, waiting for transfers between devices, local(): lax.psum_scatter(pair_part, 'col', scatter_dimension=0, tiled=False)  18.5 us
    pallas_call x2, Pallas kernels, apply_weight(): pl.pallas_call(kernel, name=name, out_shape=jax.ShapeDtypeStruct((parts,...  18.1 us
    reduce_scatter x1, waiting for transfers between devices, local(): ph_grad = lax.psum_scatter(ph_part, 'col', scatter_dimension=0, tiled=False)  13.1 us
    unnamed x16, local copies, waits for them, and re-layouts  10 us
    all_to_all x1, starting transfers between devices, local(): lax.all_to_all(outgoing, 'row', split_axis=0, concat_axis=0, tiled=True)  7.38 us
    dot_general x4, matrix products, select(): lax.dot_general(one_hot.astype(values.dtype), values, (((left_axis,), (0,...  7.13 us
    all_to_all x1, starting transfers between devices, local(): back = lax.all_to_all(back, 'row', split_axis=0, concat_axis=0, tiled=True)  5.62 us
  transfers between devices with their start and end apart: 4, of which 3 were waited for; matrix products, arithmetic and copies ran while one was open for 6% of the time, Pallas kernels for 5%

profile of v3, /device:TPU:0, one launch (start us, length us, event | category | flops | bytes accessed | tf_op | source)
XLA Modules:
  0.0 214.8 jit_solution(1206945276890288140)
XLA Ops:
  7.2 0.8 add_select_fusion.1
  8.0 2.1 select_reduce_fusion
  10.1 0.3 convert_reduce_fusion
  10.4 2.0 convolution_convert_fusion.1
  12.4 7.4 %all-to-all-start = ((bf16[16,24,256]{2,1,0:T(8,128)(2,1)}), bf16[16,24,256]{2,1,0:T(8,128)(2,1)S(1)}, u32[]{:S(2)}, u32[]{:S(2)}) async-start(bf16[16,24,256]{2,1,0:T(8,128)(2,1)} %bitcast.1), calls=%async_computation | async-start | bytes 393216 | tf_op jit(solution)/shard_map/all_to_all | solution.py:394
  19.8 0.0 reduce-scatter.5.cloned.1.call-start
  19.9 1.1 fusion.4
  21.0 0.8 select_reduce_fusion.6
  21.7 0.7 sub.26
  22.4 1.1 multiply_reduce_fusion
  23.5 1.8 pad_maximum_fusion.pair_ref
  25.3 1.2 select_reduce_fusion.1
  26.5 0.2 select_reduce_fusion.5
  26.7 0.6 select_maximum_fusion.stats_ref
  27.3 0.2 convert_reduce_fusion.1
  27.5 1.3 all-to-all-done
  28.8 0.3 convolution_convert_fusion
  29.1 1.7 pad_maximum_fusion.1.ph_ref
  30.8 101.6 %spread.1 = (bf16[16,384,512]{2,1,0:T(8,128)(2,1)}, bf16[16,384,512]{2,1,0:T(8,128)(2,1)}, bf16[2,384,512]{2,1,0:T(8,128)(2,1)}, bf16[2,384,512]{2,1,0:T(8,128)(2,1)}, f32[16,2,8,128]{3,2,1,0:T(8,128)}) custom-call(bf16[384,512]{1,0:T(8,128)(2,1)} %pad_maximum_fusion.pair_ref, bf16[384,512]{1,0:T(8,128)(2,1)} %pad_maximum_fusion.1.ph_ref, ...), custom_call_target="tpu_custom_call" | custom-call | tf_op jit(solution)/shard_map/spread/pallas_call | solution.py:313
  132.4 0.9 reduce_sum.117
  133.3 0.7 bitcast_divide_fusion
  134.0 0.1 select_reduce_fusion.3
  134.1 0.1 broadcast_in_dim.35.shift_ref
  134.2 0.0 copy-start
  134.2 1.7 copy-done
  135.9 0.0 copy-start.2
  135.9 2.8 %copy-done.2 = bf16[16,384,512]{2,1,0:T(8,128)(2,1)S(1)} copy-done((bf16[16,384,512]{2,1,0:T(8,128)(2,1)S(1)}, bf16[16,384,512]{2,1,0:T(8,128)(2,1)}, u32[]{:S(2)}) %copy-start.2) | copy-done | bytes 6291480
  138.7 0.0 copy-start.6
  138.7 1.1 copy-done.6
  139.8 0.0 copy-start.3
  139.8 0.0 copy-start.5
  139.8 8.4 %ph.1 = f32[2,384,512]{2,1,0:T(8,128)} custom-call(s32[1]{0:T(128)} %bitcast.offset_ref, bf16[2,384,512]{2,1,0:T(8,128)(2,1)S(1)} %copy-done.6, bf16[2,3072,512]{2,1,0:T(8,128)(2,1)S(1)} %bitcast.19, bf16[384,3072]{1,0:T(8,128)(2,1)S(1)} %copy-done, f32[384,1]{1,0:T(8,128)S(1)} %broadcast_in_dim.35.shift_ref), custom_call_target="tpu_custom_call" | custom-call | flops 4831838208 | bytes 11010048 | tf_op jit(solution)/shard_map/ph/pallas_call | solution.py:67
  148.2 0.0 reduce-scatter.5.cloned.1.call-update
  148.2 0.0 reduce-scatter.3.cloned.1.call-start
  148.2 0.0 copy-done.3
  148.2 0.0 copy-done.5
  148.3 0.0 copy-start.1
  148.3 2.8 %copy-done.1 = bf16[16,384,512]{2,1,0:T(8,128)(2,1)S(1)} copy-done((bf16[16,384,512]{2,1,0:T(8,128)(2,1)S(1)}, bf16[16,384,512]{2,1,0:T(8,128)(2,1)}, u32[]{:S(2)}) %copy-start.1) | copy-done | bytes 6291480
  151.0 0.0 copy-start.4
  151.0 1.7 copy-done.4
  152.7 0.0 copy-start.7
  152.7 9.7 %pair.1 = f32[2,384,512]{2,1,0:T(8,128)} custom-call(s32[1]{0:T(128)} %bitcast.offset_ref, bf16[2,384,512]{2,1,0:T(8,128)(2,1)S(1)} %copy-done.5, bf16[2,3072,512]{2,1,0:T(8,128)(2,1)S(1)} %bitcast.18, bf16[384,3072]{1,0:T(8,128)(2,1)S(1)} %copy-done.3, bf16[384,3072]{1,0:T(8,128)(2,1)S(1)} %copy-done.4), custom_call_target="tpu_custom_call" | custom-call | flops 6039797760 | bytes 11010048 | tf_op jit(solution)/shard_map/pair/pallas_call | solution.py:67
  162.4 0.0 reduce-scatter.3.cloned.1.call-update
  162.5 13.1 %reduce-scatter.5.cloned.1.call-done = f32[1,384,512]{2,1,0:T(8,128)} async-done(((f32[2,384,512]{2,1,0:T(8,128)}), f32[1,384,512]{2,1,0:T(8,128)}) %reduce-scatter.5.cloned.1.call-update) | async-done | bytes 786448 | tf_op jit(solution)/shard_map/reduce_scatter | solution.py:445
  175.5 2.5 %fusion.1 = f32[384,256]{1,0:T(8,128)} fusion(f32[384,512]{1,0:T(8,128)} %bitcast.21, s32[384]{0:T(512)S(1)} %multiply_add_fusion.1), kind=kOutput, calls=%fused_computation.10 | convolution fusion | flops 453132288 | bytes 787968 | tf_op jit(solution)/shard_map/dot_general | solution.py:349
  178.0 5.6 %all-to-all-start.1 = ((f32[16,24,256]{2,1,0:T(8,128)}), f32[16,24,256]{2,1,0:T(8,128)S(1)}, u32[]{:S(2)}, u32[]{:S(2)}) async-start(f32[16,24,256]{2,1,0:T(8,128)} %bitcast.11), calls=%async_computation.3 | async-start | bytes 786432 | tf_op jit(solution)/shard_map/all_to_all | solution.py:448
  183.7 1.8 slice_multiply_fusion
  185.5 18.5 %reduce-scatter.3.cloned.1.call-done = f32[1,384,512]{2,1,0:T(8,128)} async-done(((f32[2,384,512]{2,1,0:T(8,128)}), f32[1,384,512]{2,1,0:T(8,128)}) %reduce-scatter.3.cloned.1.call-update) | async-done | bytes 786448 | tf_op jit(solution)/shard_map/reduce_scatter | solution.py:441
  203.9 1.8 slice_multiply_fusion.1
  205.7 0.0 all-to-all-done.1
  205.7 0.0 copy-done.7
  205.7 2.3 %fusion = f32[384,256]{1,0:T(8,128)} fusion(f32[384,256]{1,0:T(8,128)S(1)} %bitcast.20, bf16[384,256]{1,0:T(8,128)(2,1)S(1)} %copy-done.7, f32[384,512]{1,0:T(8,128)} %bitcast.24, s32[384]{0:T(512)S(1)} %multiply_add_fusion, f32[384]{0:T(512)S(1)} %broadcast_multiply_fusion), kind=kOutput, calls=%fused_computation.2 | convolution fusion | flops 453722112 | bytes 1379328 | tf_op jit(solution)/shard_map/dot_general | solution.py:349
  (5 shorter events, 0.0 us)
Async XLA Ops:
  12.4 16.3 %all-to-all-start = ((bf16[16,24,256]{2,1,0:T(8,128)(2,1)}), bf16[16,24,256]{2,1,0:T(8,128)(2,1)S(1)}, u32[]{:S(2)}, u32[]{:S(2)}) async-start(bf16[16,24,256]{2,1,0:T(8,128)(2,1)} %bitcast.1), calls=%async_computation | async-start | bytes 393216 | tf_op jit(solution)/shard_map/all_to_all | solution.py:394
  19.8 155.7 %reduce-scatter.5.cloned.1.call-start = ((), (), s32[]{:S(2)}) async-start(), calls=%async_computation.5 | async-start | bytes 2359296 | tf_op jit(solution)/shard_map/reduce_scatter | solution.py:445
  134.2 1.7 copy-start
  135.9 2.8 %copy-start.2 = (bf16[16,384,512]{2,1,0:T(8,128)(2,1)S(1)}, bf16[16,384,512]{2,1,0:T(8,128)(2,1)}, u32[]{:S(2)}) copy-start(bf16[16,384,512]{2,1,0:T(8,128)(2,1)} %get-tuple-element.12) | copy-start | bytes 18874372
  138.7 1.1 copy-start.6
  139.8 8.4 %copy-start.3 = (bf16[384,3072]{1,0:T(8,128)(2,1)S(1)}, bf16[384,3072]{1,0:T(8,128)(2,1)}, u32[]{:S(2)}) copy-start(bf16[384,3072]{1,0:T(8,128)(2,1)} %mult_ref.2) | copy-start | bytes 7077892
  139.8 8.5 %copy-start.5 = (bf16[2,384,512]{2,1,0:T(8,128)(2,1)S(1)}, bf16[2,384,512]{2,1,0:T(8,128)(2,1)}, u32[]{:S(2)}) copy-start(bf16[2,384,512]{2,1,0:T(8,128)(2,1)} %get-tuple-element.8.own_ref) | copy-start | bytes 2359300
  148.2 55.8 %reduce-scatter.3.cloned.1.call-start = ((), (), s32[]{:S(2)}) async-start(), calls=%async_computation.4 | async-start | bytes 2359296 | tf_op jit(solution)/shard_map/reduce_scatter | solution.py:441
  148.3 2.8 %copy-start.1 = (bf16[16,384,512]{2,1,0:T(8,128)(2,1)S(1)}, bf16[16,384,512]{2,1,0:T(8,128)(2,1)}, u32[]{:S(2)}) copy-start(bf16[16,384,512]{2,1,0:T(8,128)(2,1)} %get-tuple-element.9) | copy-start | bytes 18874372
  151.0 1.7 copy-start.4
  152.7 53.0 %copy-start.7 = (bf16[384,256]{1,0:T(8,128)(2,1)S(1)}, bf16[384,256]{1,0:T(8,128)(2,1)}, u32[]{:S(2)}) copy-start(bf16[384,256]{1,0:T(8,128)(2,1)} %param.8) | copy-start | bytes 589828
  178.0 27.7 %all-to-all-start.1 = ((f32[16,24,256]{2,1,0:T(8,128)}), f32[16,24,256]{2,1,0:T(8,128)S(1)}, u32[]{:S(2)}, u32[]{:S(2)}) async-start(f32[16,24,256]{2,1,0:T(8,128)} %bitcast.11), calls=%async_computation.3 | async-start | bytes 786432 | tf_op jit(solution)/shard_map/all_to_all | solution.py:448
Sparse Core Ops, SparseCore 0:
  148.3 27.1 reduce-scatter.4
  177.8 26.1 reduce-scatter.2

commit v4 on v3

--- a/solution.py
+++ b/solution.py
@@ -11,85 +11,6 @@
 penalty = 2.5
 
 
-def tile_weight(offset_ref, own_ref, cols_ref, mult_ref, shift):
-    parts, block, _ = own_ref.shape
-    tile = cols_ref.shape[1]
-    gram = None
-    for part in range(parts):
-        term = lax.dot_general(
-            own_ref[part],
-            cols_ref[part],
-            (((1,), (1,)), ((), ())),
-            preferred_element_type=jnp.float32,
-        )
-        gram = term if gram is None else gram + term
-    rows = lax.broadcasted_iota(jnp.int32, (block, tile), 0) + offset_ref[0]
-    cols = lax.broadcasted_iota(jnp.int32, (block, tile), 1) + pl.program_id(0) * tile
-    resid = jnp.where(rows == cols, shift, 0.0) - gram
-    return (mult_ref[...].astype(jnp.float32) + penalty * resid).astype(jnp.bfloat16)
-
-
-def pair_kernel(offset_ref, own_ref, cols_ref, mult_ref, ham_ref, out_ref):
-    @pl.when(pl.program_id(0) == 0)
-    def _():
-        out_ref[...] = jnp.zeros_like(out_ref)
-
-    half = own_ref.shape[2] // 2
-    weight = tile_weight(offset_ref, own_ref, cols_ref, mult_ref, shift_value)
-    for part in range(own_ref.shape[0]):
-        first = cols_ref[part, :, :half]
-        out_ref[part, :, :half] += jnp.dot(
-            ham_ref[...], first, preferred_element_type=jnp.float32
-        ) - jnp.dot(weight, first, preferred_element_type=jnp.float32)
-        out_ref[part, :, half:] -= jnp.dot(
-            weight, cols_ref[part, :, half:], preferred_element_type=jnp.float32
-        )
-
-
-def ph_kernel(offset_ref, own_ref, cols_ref, mult_ref, shift_ref, out_ref):
-    @pl.when(pl.program_id(0) == 0)
-    def _():
-        out_ref[...] = jnp.zeros_like(out_ref)
-
-    weight = tile_weight(offset_ref, own_ref, cols_ref, mult_ref, shift_ref[...])
-    for part in range(own_ref.shape[0]):
-        out_ref[part] -= jnp.dot(weight, cols_ref[part], preferred_element_type=jnp.float32)
-
-
-def apply_weight(kernel, name, offset, own, cols, mult, extra, extra_tiled):
-    parts, block, depth = own.shape
-    width = cols.shape[1]
-    tile = 512 if width % 512 == 0 else 256
-    if extra_tiled:
-        extra_spec = pl.BlockSpec((block, tile), lambda j, o: (0, j))
-    else:
-        extra_spec = pl.BlockSpec(extra.shape, lambda j, o: (0, 0))
-    return pl.pallas_call(
-        kernel,
-        name=name,
-        out_shape=jax.ShapeDtypeStruct((parts, block, depth), jnp.float32),
-        grid_spec=pltpu.PrefetchScalarGridSpec(
-            num_scalar_prefetch=1,
-            grid=(width // tile,),
-            in_specs=[
-                pl.BlockSpec((parts, block, depth), lambda j, o: (0, 0, 0)),
-                pl.BlockSpec((parts, tile, depth), lambda j, o: (0, j, 0)),
-                pl.BlockSpec((block, tile), lambda j, o: (0, j)),
-                extra_spec,
-            ],
-            out_specs=pl.BlockSpec((parts, block, depth), lambda j, o: (0, 0, 0)),
-        ),
-        compiler_params=pltpu.CompilerParams(
-            dimension_semantics=("arbitrary",), vmem_limit_bytes=40 << 20
-        ),
-        cost_estimate=pl.CostEstimate(
-            flops=(5 if extra_tiled else 4) * block * width * parts * depth,
-            bytes_accessed=2 * width * (parts * depth + 2 * block),
-            transcendentals=0,
-        ),
-    )(offset, own, cols, mult, extra)
-
-
 MESH = pl.DeviceIdType.MESH
 
 
@@ -99,11 +20,26 @@
     pair_ref,
     ph_ref,
     stats_ref,
+    member_ref,
+    lengths_ref,
+    ham_hbm,
+    mult_q_hbm,
+    mult_g_hbm,
+    pair_out,
+    ph_out,
+    sums_out,
     pair_cols,
     ph_cols,
     pair_own,
     ph_own,
     stats_all,
+    ham,
+    mult_q,
+    mult_g,
+    pair_acc,
+    ph_acc,
+    pair_in,
+    ph_in,
     place_send,
     place_recv,
     own_send,
@@ -117,6 +53,9 @@
     stats_recv,
     rows_send,
     rows_recv,
+    fetch_sem,
+    swap_send,
+    swap_recv,
 ):
     row = lax.axis_index("row")
     col = lax.axis_index("col")
@@ -255,8 +194,7 @@
     for d in range(1, groups):
         stats_rows(d, row).start()
 
-    for a in range(2):
-
+    def launch(a):
         @pl.when(moved)
         def _():
             placing(a).wait_recv()
@@ -268,77 +206,207 @@
         for way in range(2):
             ring(a, way, 1, 0).start()
         mating(a, 0, 0, core).start()
-
-    for a in range(2):
         for d in range(1, col_groups):
             owning(a, d, col).start()
 
+    def arrive(a, step):
+        for way in range(2):
+            ring(a, way, step, step).wait_recv()
+            if step < half:
+                ring(a, way, step + 1, step).start()
+            mating(a, way, step, core).start()
+
+    def settle(a):
+        mating(a, 0, 0, 1 - core).wait_recv()
+        for step in range(1, half + 1):
+            for way in range(2):
+                mating(a, way, step, 1 - core).wait_recv()
+        for d in range(1, col_groups):
+            owning(a, d, (col + col_groups - d) % col_groups).wait_recv()
+        keeping(a).wait()
+
+    def drain(a):
+        mating(a, 0, 0, core).wait_send()
+        for step in range(1, half + 1):
+            for way in range(2):
+                mating(a, way, step, core).wait_send()
+                ring(a, way, step, step - 1).wait_send()
+        for d in range(1, col_groups):
+            owning(a, d, col).wait_send()
+
+        @pl.when(moved)
+        def _():
+            placing(a).wait_send()
+
+    accs_ = [pair_acc, ph_acc]
+    ins_ = [pair_in, ph_in]
+
+    def swapping(a, d):
+        return pltpu.make_async_remote_copy(
+            src_ref=accs_[a].at[(col + d) % col_groups],
+            dst_ref=ins_[a].at[d - 1],
+            send_sem=swap_send.at[a, d - 1],
+            recv_sem=swap_recv.at[a, d - 1],
+            device_id=peers[d - 1],
+            device_id_type=MESH,
+        )
+
+    def finish(a, out):
+        total = accs_[a][col]
+        for d in range(1, col_groups):
+            swapping(a, d).wait_recv()
+            total = total + ins_[a][d - 1]
+        out[...] = 2.0 * total
+
+    depth = pair_ref.shape[1]
+    joined = 2 if per % 2 == 0 else 1
+    tile = joined * block
+    tiles = per // joined
+    offset = row * block - col * per * block
+
+    def weighted(a, t, mult, shift):
+        gram = None
+        tiles_of = []
+        for part in range(col_groups):
+            there = cols_[a][pl.ds(part * per + t * joined, joined)].reshape(tile, depth)
+            tiles_of.append(there)
+            term = lax.dot_general(
+                owns_[a][part],
+                there,
+                (((1,), (1,)), ((), ())),
+                preferred_element_type=jnp.float32,
+            )
+            gram = term if gram is None else gram + term
+        rows = lax.broadcasted_iota(jnp.int32, (block, tile), 0) + offset
+        places = lax.broadcasted_iota(jnp.int32, (block, tile), 1) + t * tile
+        resid = jnp.where(rows == places, shift, 0.0) - gram
+        span = pl.ds(pl.multiple_of(t * tile, 128), tile)
+        full = mult[:, span].astype(jnp.float32) + penalty * resid
+        return full.astype(jnp.bfloat16), tiles_of, span
+
+    def pair_tiles(first, last):
+        @pl.loop(first, last)
+        def _(t):
+            weight, tiles_of, span = weighted(0, t, mult_q, shift_value)
+            for part in range(col_groups):
+                left = tiles_of[part][:, : depth // 2]
+                right = tiles_of[part][:, depth // 2 :]
+                pair_acc[part, :, : depth // 2] += jnp.dot(
+                    ham[:, span], left, preferred_element_type=jnp.float32
+                ) - jnp.dot(weight, left, preferred_element_type=jnp.float32)
+                pair_acc[part, :, depth // 2 :] -= jnp.dot(
+                    weight, right, preferred_element_type=jnp.float32
+                )
+
+    def ph_tiles(shift):
+        @pl.loop(0, tiles)
+        def _(t):
+            weight, tiles_of, _span = weighted(1, t, mult_g, shift)
+            for part in range(col_groups):
+                ph_acc[part] -= jnp.dot(
+                    weight, tiles_of[part], preferred_element_type=jnp.float32
+                )
+
+    fetches = [
+        pltpu.make_async_copy(mult_q_hbm, mult_q, fetch_sem.at[0]),
+        pltpu.make_async_copy(ham_hbm, ham, fetch_sem.at[1]),
+        pltpu.make_async_copy(mult_g_hbm, mult_g, fetch_sem.at[2]),
+    ]
+    lag = min(2, half)
+
+    launch(0)
+    for fetch in fetches:
+        fetch.start()
+    pair_acc[...] = jnp.zeros_like(pair_acc)
+    ph_acc[...] = jnp.zeros_like(ph_acc)
     for step in range(1, half + 1):
-        for a in range(2):
-            for way in range(2):
-                ring(a, way, step, step).wait_recv()
-                if step < half:
-                    ring(a, way, step + 1, step).start()
-                mating(a, way, step, core).start()
+        arrive(0, step)
+        if step == lag:
+            launch(1)
+        if step > lag:
+            arrive(1, step - lag)
+    settle(0)
+    fetches[0].wait()
+    fetches[1].wait()
+    for k in range(lag):
+        pair_tiles(tiles * k // lag, tiles * (k + 1) // lag)
+        arrive(1, half - lag + 1 + k)
+    for d in range(1, col_groups):
+        swapping(0, d).start()
 
     for d in range(1, col_groups):
         stats_over(d, col).wait_send()
     for d in range(1, groups):
         stats_rows(d, (row + groups - d) % groups).wait_recv()
         stats_rows(d, row).wait_send()
+    sums = jnp.sum(stats_all[...].reshape((groups * col_groups,) + stats_ref.shape), axis=0)
+    sums_out[...] = sums
+    means = 2.0 * sums[0:1] / lengths_ref[0:1]
+    shift = jnp.sum(member_ref[...] * means, axis=1, keepdims=True)
+
+    settle(1)
+    fetches[2].wait()
+    ph_tiles(shift)
+    finish(0, pair_out)
+    for d in range(1, col_groups):
+        swapping(1, d).start()
+    drain(0)
+    drain(1)
+    finish(1, ph_out)
     for a in range(2):
-        mating(a, 0, 0, 1 - core).wait_recv()
-        mating(a, 0, 0, core).wait_send()
-        for step in range(1, half + 1):
-            for way in range(2):
-                mating(a, way, step, 1 - core).wait_recv()
-                mating(a, way, step, core).wait_send()
-                ring(a, way, step, step - 1).wait_send()
         for d in range(1, col_groups):
-            owning(a, d, (col + col_groups - d) % col_groups).wait_recv()
-            owning(a, d, col).wait_send()
-        keeping(a).wait()
-
-        @pl.when(moved)
-        def _():
-            placing(a).wait_send()
-
-
-def spread(groups, col_groups, pair_local, ph_local, stats):
+            swapping(a, d).wait_send()
+
+
+def spread(groups, col_groups, pair_local, ph_local, stats, member, lengths, ham, mult_q, mult_g):
     block, depth = pair_local.shape
     half = groups // 4
+    over = max(col_groups - 1, 1)
     dma = pltpu.SemaphoreType.DMA
-    cols = jax.ShapeDtypeStruct((groups, block, depth), pair_local.dtype)
-    own = jax.ShapeDtypeStruct((col_groups, block, depth), pair_local.dtype)
+    kind = pair_local.dtype
+    grad = jax.ShapeDtypeStruct((block, depth), jnp.float32)
+    vmem = pl.BlockSpec(memory_space=pltpu.VMEM)
+    hbm = pl.BlockSpec(memory_space=pl.ANY)
     return pl.pallas_call(
         functools.partial(spread_kernel, groups, col_groups),
         name="spread",
-        out_shape=(
-            cols,
-            cols,
-            own,
-            own,
-            jax.ShapeDtypeStruct((groups, col_groups) + stats.shape, stats.dtype),
-        ),
-        in_specs=[pl.BlockSpec(memory_space=pltpu.VMEM)] * 3,
-        out_specs=(pl.BlockSpec(memory_space=pl.ANY),) * 5,
+        out_shape=(grad, grad, jax.ShapeDtypeStruct(stats.shape, stats.dtype)),
+        in_specs=[vmem] * 5 + [hbm] * 3,
+        out_specs=(vmem,) * 3,
         scratch_shapes=[
+            pltpu.VMEM((groups, block, depth), kind),
+            pltpu.VMEM((groups, block, depth), kind),
+            pltpu.VMEM((col_groups, block, depth), kind),
+            pltpu.VMEM((col_groups, block, depth), kind),
+            pltpu.VMEM((groups, col_groups) + stats.shape, stats.dtype),
+            pltpu.VMEM(ham.shape, ham.dtype),
+            pltpu.VMEM(mult_q.shape, mult_q.dtype),
+            pltpu.VMEM(mult_g.shape, mult_g.dtype),
+            pltpu.VMEM((col_groups, block, depth), jnp.float32),
+            pltpu.VMEM((col_groups, block, depth), jnp.float32),
+            pltpu.VMEM((over, block, depth), jnp.float32),
+            pltpu.VMEM((over, block, depth), jnp.float32),
             dma((2,)),
             dma((2,)),
-            dma((2, max(col_groups - 1, 1))),
-            dma((2, max(col_groups - 1, 1))),
+            dma((2, over)),
+            dma((2, over)),
             dma((2, 2, half)),
             dma((2, 2, half)),
             dma((2, 2, half + 1)),
             dma((2, 2, half + 1)),
             dma((2, 3)),
-            dma((max(col_groups - 1, 1),)),
-            dma((max(col_groups - 1, 1),)),
+            dma((over,)),
+            dma((over,)),
             dma((groups - 1,)),
             dma((groups - 1,)),
+            dma((3,)),
+            dma((2, over)),
+            dma((2, over)),
         ],
-        compiler_params=pltpu.CompilerParams(collective_id=0, has_side_effects=True),
-    )(pair_local, ph_local, stats)
+        compiler_params=pltpu.CompilerParams(
+            collective_id=0, has_side_effects=True, vmem_limit_bytes=56 << 20
+        ),
+    )(pair_local, ph_local, stats, member, lengths, ham, mult_q, mult_g)
 
 
 def select(one_hot, values, left_axis):
@@ -423,37 +491,33 @@
         ]
     )
     stats = jnp.pad(sums, ((0, 6), (0, -count % 128)))
-    pair_cols, ph_cols, pair_own, ph_own, stats_all = spread(
-        groups, col_groups, pair_local, ph_local, stats
+    lanes = ((0, 0), (0, -count % 128))
+    pair_grad, ph_grad, sums = spread(
+        groups,
+        col_groups,
+        pair_local,
+        ph_local,
+        stats,
+        jnp.pad(member_ph, lanes),
+        jnp.pad(jnp.broadcast_to(lengths, (8, count)), lanes, constant_values=1.0),
+        hamiltonian,
+        multiplier_q,
+        multiplier_g,
     )
-    sums = jnp.sum(stats_all, axis=(0, 1))[:, :count]
-    shift_means = 2.0 * sums[0] / lengths
+    sums = sums[:, :count]
     scale_means = 2.0 * (sums[1] + penalty * sums[0]) / lengths
-    shift_rows = jnp.sum(member_ph * shift_means[None, :], axis=1)
     scale_rows = jnp.sum(member * scale_means[None, :], axis=1)
-
-    pair_cols = pair_cols.reshape(col_groups, width, 2 * rank_part)
-    ph_cols = ph_cols.reshape(col_groups, width, 2 * rank_part)
-    offsets = offset.reshape(1)
-    pair_part = apply_weight(
-        pair_kernel, "pair", offsets, pair_own, pair_cols, multiplier_q, hamiltonian, True
-    )
-    pair_grad = lax.psum_scatter(pair_part, "col", scatter_dimension=0, tiled=False)
-    ph_part = apply_weight(
-        ph_kernel, "ph", offsets, ph_own, ph_cols, multiplier_g, shift_rows[:, None], False
-    )
-    ph_grad = lax.psum_scatter(ph_part, "col", scatter_dimension=0, tiled=False)
 
     back = select(take_hot, ph_grad[:, :rank_part], 0)
     back = lax.all_to_all(back, "row", split_axis=0, concat_axis=0, tiled=True)
     returned = select(send_hot, back, 1)
     grad_density = (
-        2.0 * pair_grad[:, :rank_part]
+        pair_grad[:, :rank_part]
         + 2.0 * scale_rows[:, None] * density_factor.astype(jnp.float32)
-        + 2.0 * returned
+        + returned
     )
-    grad_hole = 2.0 * pair_grad[:, rank_part:]
-    grad_ph = 2.0 * ph_grad[:, rank_part:]
+    grad_hole = pair_grad[:, rank_part:]
+    grad_ph = ph_grad[:, rank_part:]
     return (grad_density, grad_hole, grad_ph)
 
 

time: 216 us -> 186 us (0.86)
  waiting for transfers between devices: 32.8 us -> 8.92 us
  Pallas kernels: 120 us -> 141 us
  between operations: 14.2 us -> 0.78 us
  local copies, waits for them, and re-layouts: 10.1 us -> 3.16 us
  other arithmetic: 17.8 us -> 13.6 us
  starting transfers between devices: 13.1 us -> 10.9 us
    pallas_call x1, Pallas kernels: 102 us -> 141 us  [spread(): pl.pallas_call(functools.partial(spread_kernel, groups, col_groups), name...]
    reduce_scatter x2 -> x0, waiting for transfers between devices: 31.5 us -> none  [the longest x1 18.5 us: local(): lax.psum_scatter(pair_part, 'col', scatter_dimension=0, tiled=False)]
    pallas_call x2 -> x0, Pallas kernels: 18.1 us -> none  [apply_weight(): pl.pallas_call(kernel, name=name, out_shape=jax.ShapeDtypeStruct((parts,...]
    unnamed x16 -> x8, local copies, waits for them, and re-layouts: 10 us -> 0.02 us
    all_to_all x1, waiting for transfers between devices: 0.01 us -> 8.59 us  [local(): back = lax.all_to_all(back, 'row', split_axis=0, concat_axis=0, tiled=True)]
    mul x2 -> x0, other arithmetic: 3.6 us -> none  [the longest x1 1.83 us: local(): grad_ph = 2.0 * ph_grad[:, rank_part:]]
    slice x0 -> x2, local copies, waits for them, and re-layouts: none -> 2.54 us  [the longest x1 1.77 us: local(): grad_ph = ph_grad[:, rank_part:]]
  transfers between devices with their start and end apart: 4 -> 2, of which waited for: 3 -> 2; matrix products, arithmetic and copies ran while one was open for 6% -> 7% of each run, Pallas kernels for 5% -> 0%
where the time goes in v4:
time: 186 us; the launch traced here: 185 us
  Pallas kernels  141 us (76%)
  other arithmetic  13.6 us (7%)
  starting transfers between devices  10.9 us (6%)
  waiting for transfers between devices  8.92 us (5%)
  matrix products  6.22 us (3%)
  local copies, waits for them, and re-layouts  3.16 us (2%)
    pallas_call x1, Pallas kernels, spread(): pl.pallas_call(functools.partial(spread_kernel, groups, col_groups), name...  141 us
    all_to_all x1, waiting for transfers between devices, local(): back = lax.all_to_all(back, 'row', split_axis=0, concat_axis=0, tiled=True)  8.59 us
    all_to_all x1, starting transfers between devices, local(): lax.all_to_all(outgoing, 'row', split_axis=0, concat_axis=0, tiled=True)  7.38 us
    dot_general x4, matrix products, select(): lax.dot_general(one_hot.astype(values.dtype), values, (((left_axis,), (0,...  6.22 us
  transfers between devices with their start and end apart: 2, of which 2 were waited for; matrix products, arithmetic and copies ran while one was open for 7% of the time, Pallas kernels for 0%

profile of v4, /device:TPU:0, one launch (start us, length us, event | category | flops | bytes accessed | tf_op | source)
XLA Modules:
  0.0 185.0 jit_solution(7742591356459757972)
XLA Ops:
  0.6 0.0 copy-start.2
  0.6 0.8 add_select_fusion.1
  1.5 2.1 %select_reduce_fusion = s32[384]{0:T(512)S(1)} fusion(s32[6144]{0:T(1024)} %param.14, s32[384]{0:T(512)S(1)} %get-tuple-element.15), kind=kLoop, calls=%fused_computation | loop fusion | flops 7077504 | bytes 27648 | tf_op jit(solution)/shard_map/reduce_sum | solution.py:452
  3.6 0.3 convert_reduce_fusion
  3.9 2.0 %convolution_convert_fusion.1 = bf16[384,256]{1,0:T(8,128)(2,1)} fusion(bf16[384,256]{1,0:T(8,128)(2,1)} %param.8, s32[384]{0:T(512)S(1)} %multiply_add_fusion), kind=kOutput, calls=%fused_computation.3 | convolution fusion | flops 75743232 | bytes 394752 | tf_op jit(solution)/shard_map/dot_general | solution.py:417
  6.0 7.4 %all-to-all-start = ((bf16[16,24,256]{2,1,0:T(8,128)(2,1)}), bf16[16,24,256]{2,1,0:T(8,128)(2,1)S(1)}, u32[]{:S(2)}, u32[]{:S(2)}) async-start(bf16[16,24,256]{2,1,0:T(8,128)(2,1)} %bitcast), calls=%async_computation | async-start | bytes 393216 | tf_op jit(solution)/shard_map/all_to_all | solution.py:462
  13.4 1.1 fusion.3
  14.4 0.8 select_reduce_fusion.5
  15.2 0.7 fusion.12
  15.9 1.1 multiply_reduce_fusion
  17.0 0.1 compare_and_fusion
  17.1 0.7 pad_convert_fusion.member_ref
  17.8 1.8 pad_maximum_fusion.pair_ref
  19.6 1.2 select_reduce_fusion.1
  20.8 0.3 select_reduce_fusion.4
  21.1 0.6 select_maximum_fusion.stats_ref
  21.7 0.2 convert_reduce_fusion.1
  22.0 0.3 all-to-all-done
  22.3 0.3 convolution_convert_fusion
  22.6 0.0 copy-done.2
  22.6 0.8 pad_maximum_fusion.1.ph_ref
  23.4 0.6 pad.20.lengths_ref
  24.0 141.4 %spread.1 = (f32[384,512]{1,0:T(8,128)}, f32[384,512]{1,0:T(8,128)}, f32[8,128]{1,0:T(8,128)}) custom-call(bf16[384,512]{1,0:T(8,128)(2,1)} %pad_maximum_fusion.pair_ref, bf16[384,512]{1,0:T(8,128)(2,1)} %pad_maximum_fusion.1.ph_ref, f32[8,128]{1,0:T(8,128)} %select_maximum_fusion.stats_ref, f32[384,128]{1,0:T(8,128)} %pad_convert_fusion.member_ref, ...), custom_call_target="tpu_custom_call" | custom-call | tf_op jit(solution)/shard_map/spread/pallas_call | solution.py:370
  165.4 0.0 copy-start.1
  165.4 0.0 copy-start.3
  165.5 0.0 copy-start
  165.5 2.6 %fusion = f32[384,256]{1,0:T(8,128)} fusion(f32[384,512]{1,0:T(8,128)} %get-tuple-element.8, s32[384]{0:T(512)S(1)} %multiply_add_fusion.1), kind=kOutput, calls=%fused_computation.9 | convolution fusion | flops 453132288 | bytes 787968 | tf_op jit(solution)/shard_map/dot_general | solution.py:417
  168.1 3.6 %all-to-all-start.1 = ((f32[16,24,256]{2,1,0:T(8,128)}), f32[16,24,256]{2,1,0:T(8,128)S(1)}, u32[]{:S(2)}, u32[]{:S(2)}) async-start(f32[16,24,256]{2,1,0:T(8,128)} %bitcast.5), calls=%async_computation.1 | async-start | bytes 786432 | tf_op jit(solution)/shard_map/all_to_all | solution.py:512
  171.6 1.8 slice.26
  173.4 0.0 copy-done.1
  173.4 0.8 slice.25
  174.2 0.0 copy-done.3
  174.2 0.8 bitcast_divide_fusion
  174.9 0.2 select_reduce_fusion.2
  175.2 8.6 %all-to-all-done.1 = f32[16,24,256]{2,1,0:T(8,128)S(1)} async-done(((f32[16,24,256]{2,1,0:T(8,128)}), f32[16,24,256]{2,1,0:T(8,128)S(1)}, u32[]{:S(2)}, u32[]{:S(2)}) %all-to-all-start.1) | async-done | bytes 393248 | tf_op jit(solution)/shard_map/all_to_all | solution.py:512
  183.7 0.0 copy-done
  183.8 1.3 convolution_add_fusion
  (6 shorter events, 0.1 us)
Async XLA Ops:
  0.6 22.0 %copy-start.2 = (bf16[384,256]{1,0:T(8,128)(2,1)S(1)}, bf16[384,256]{1,0:T(8,128)(2,1)}, u32[]{:S(2)}) copy-start(bf16[384,256]{1,0:T(8,128)(2,1)} %param.10) | copy-start | bytes 589828
  6.0 16.3 %all-to-all-start = ((bf16[16,24,256]{2,1,0:T(8,128)(2,1)}), bf16[16,24,256]{2,1,0:T(8,128)(2,1)S(1)}, u32[]{:S(2)}, u32[]{:S(2)}) async-start(bf16[16,24,256]{2,1,0:T(8,128)(2,1)} %bitcast), calls=%async_computation | async-start | bytes 393216 | tf_op jit(solution)/shard_map/all_to_all | solution.py:462
  165.4 7.9 %copy-start.1 = (f32[384,512]{1,0:T(8,128)S(1)}, f32[384,512]{1,0:T(8,128)}, u32[]{:S(2)}) copy-start(f32[384,512]{1,0:T(8,128)} %get-tuple-element.6) | copy-start | bytes 2359300
  165.4 8.7 %copy-start.3 = (s32[48]{0:T(128)S(1)}, s32[48]{0:T(128)}, u32[]{:S(2)}) copy-start(s32[48]{0:T(128)} %param.15) | copy-start | bytes 580
  165.5 18.3 %copy-start = (bf16[384,256]{1,0:T(8,128)(2,1)S(1)}, bf16[384,256]{1,0:T(8,128)(2,1)}, u32[]{:S(2)}) copy-start(bf16[384,256]{1,0:T(8,128)(2,1)} %param.8) | copy-start | bytes 589828
  168.1 15.7 %all-to-all-start.1 = ((f32[16,24,256]{2,1,0:T(8,128)}), f32[16,24,256]{2,1,0:T(8,128)S(1)}, u32[]{:S(2)}, u32[]{:S(2)}) async-start(f32[16,24,256]{2,1,0:T(8,128)} %bitcast.5), calls=%async_computation.1 | async-start | bytes 786432 | tf_op jit(solution)/shard_map/all_to_all | solution.py:512

commit v5 on v4

--- a/solution.py
+++ b/solution.py
@@ -176,8 +176,7 @@
     stats_here().start()
     for d in range(1, col_groups):
         stats_over(d, col).start()
-    for a in range(2):
-
+    def place(a):
         @pl.when(moved)
         def _():
             placing(a).start()
@@ -187,6 +186,8 @@
             staying(a).start()
 
         keeping(a).start()
+
+    place(0)
 
     stats_here().wait()
     for d in range(1, col_groups):
@@ -206,6 +207,8 @@
         for way in range(2):
             ring(a, way, 1, 0).start()
         mating(a, 0, 0, core).start()
+
+    def lend(a):
         for d in range(1, col_groups):
             owning(a, d, col).start()
 
@@ -241,22 +244,25 @@
     accs_ = [pair_acc, ph_acc]
     ins_ = [pair_in, ph_in]
 
-    def swapping(a, d):
-        return pltpu.make_async_remote_copy(
-            src_ref=accs_[a].at[(col + d) % col_groups],
-            dst_ref=ins_[a].at[d - 1],
-            send_sem=swap_send.at[a, d - 1],
-            recv_sem=swap_recv.at[a, d - 1],
+    every = slice(0, block)
+    halves = [slice(0, block // 2), slice(block // 2, block)]
+
+    def swapping(a, d, slot, rows):
+        return pltpu.make_async_remote_copy(
+            src_ref=accs_[a].at[(col + d) % col_groups, rows],
+            dst_ref=ins_[a].at[d - 1, rows],
+            send_sem=swap_send.at[slot, d - 1],
+            recv_sem=swap_recv.at[slot, d - 1],
             device_id=peers[d - 1],
             device_id_type=MESH,
         )
 
-    def finish(a, out):
-        total = accs_[a][col]
+    def finish(a, out, slot, rows):
+        total = accs_[a][col, rows]
         for d in range(1, col_groups):
-            swapping(a, d).wait_recv()
-            total = total + ins_[a][d - 1]
-        out[...] = 2.0 * total
+            swapping(a, d, slot, rows).wait_recv()
+            total = total + ins_[a][d - 1, rows]
+        out[rows] = 2.0 * total
 
     depth = pair_ref.shape[1]
     joined = 2 if per % 2 == 0 else 1
@@ -264,30 +270,31 @@
     tiles = per // joined
     offset = row * block - col * per * block
 
-    def weighted(a, t, mult, shift):
+    def weighted(a, t, mult, shift, taken):
         gram = None
         tiles_of = []
         for part in range(col_groups):
             there = cols_[a][pl.ds(part * per + t * joined, joined)].reshape(tile, depth)
             tiles_of.append(there)
             term = lax.dot_general(
-                owns_[a][part],
+                owns_[a][part, taken],
                 there,
                 (((1,), (1,)), ((), ())),
                 preferred_element_type=jnp.float32,
             )
             gram = term if gram is None else gram + term
-        rows = lax.broadcasted_iota(jnp.int32, (block, tile), 0) + offset
-        places = lax.broadcasted_iota(jnp.int32, (block, tile), 1) + t * tile
+        dims = (taken.stop - taken.start, tile)
+        rows = lax.broadcasted_iota(jnp.int32, dims, 0) + (offset + taken.start)
+        places = lax.broadcasted_iota(jnp.int32, dims, 1) + t * tile
         resid = jnp.where(rows == places, shift, 0.0) - gram
         span = pl.ds(pl.multiple_of(t * tile, 128), tile)
-        full = mult[:, span].astype(jnp.float32) + penalty * resid
+        full = mult[taken, span].astype(jnp.float32) + penalty * resid
         return full.astype(jnp.bfloat16), tiles_of, span
 
     def pair_tiles(first, last):
         @pl.loop(first, last)
         def _(t):
-            weight, tiles_of, span = weighted(0, t, mult_q, shift_value)
+            weight, tiles_of, span = weighted(0, t, mult_q, shift_value, every)
             for part in range(col_groups):
                 left = tiles_of[part][:, : depth // 2]
                 right = tiles_of[part][:, depth // 2 :]
@@ -298,12 +305,12 @@
                     weight, right, preferred_element_type=jnp.float32
                 )
 
-    def ph_tiles(shift):
+    def ph_tiles(shift, taken):
         @pl.loop(0, tiles)
         def _(t):
-            weight, tiles_of, _span = weighted(1, t, mult_g, shift)
+            weight, tiles_of, _span = weighted(1, t, mult_g, shift[taken], taken)
             for part in range(col_groups):
-                ph_acc[part] -= jnp.dot(
+                ph_acc[part, taken] -= jnp.dot(
                     weight, tiles_of[part], preferred_element_type=jnp.float32
                 )
 
@@ -315,14 +322,18 @@
     lag = min(2, half)
 
     launch(0)
+    place(1)
     for fetch in fetches:
         fetch.start()
     pair_acc[...] = jnp.zeros_like(pair_acc)
     ph_acc[...] = jnp.zeros_like(ph_acc)
     for step in range(1, half + 1):
         arrive(0, step)
+        if step == 1:
+            lend(0)
         if step == lag:
             launch(1)
+            lend(1)
         if step > lag:
             arrive(1, step - lag)
     settle(0)
@@ -332,7 +343,7 @@
         pair_tiles(tiles * k // lag, tiles * (k + 1) // lag)
         arrive(1, half - lag + 1 + k)
     for d in range(1, col_groups):
-        swapping(0, d).start()
+        swapping(0, d, 0, every).start()
 
     for d in range(1, col_groups):
         stats_over(d, col).wait_send()
@@ -346,16 +357,21 @@
 
     settle(1)
     fetches[2].wait()
-    ph_tiles(shift)
-    finish(0, pair_out)
+    for h in range(2):
+        ph_tiles(shift, halves[h])
+        if h == 0:
+            drain(0)
+        else:
+            finish(0, pair_out, 0, every)
+        for d in range(1, col_groups):
+            swapping(1, d, 1 + h, halves[h]).start()
+    drain(1)
+    for h in range(2):
+        finish(1, ph_out, 1 + h, halves[h])
     for d in range(1, col_groups):
-        swapping(1, d).start()
-    drain(0)
-    drain(1)
-    finish(1, ph_out)
-    for a in range(2):
-        for d in range(1, col_groups):
-            swapping(a, d).wait_send()
+        swapping(0, d, 0, every).wait_send()
+        for h in range(2):
+            swapping(1, d, 1 + h, halves[h]).wait_send()
 
 
 def spread(groups, col_groups, pair_local, ph_local, stats, member, lengths, ham, mult_q, mult_g):
@@ -400,8 +416,8 @@
             dma((groups - 1,)),
             dma((groups - 1,)),
             dma((3,)),
-            dma((2, over)),
-            dma((2, over)),
+            dma((3, over)),
+            dma((3, over)),
         ],
         compiler_params=pltpu.CompilerParams(
             collective_id=0, has_side_effects=True, vmem_limit_bytes=56 << 20

time: 186 us -> 185 us (level)
  no operation moved by 1% of the time
where the time goes in v5:
time: 185 us
  Pallas kernels  140 us (76%)
  other arithmetic  13.6 us (7%)
  starting transfers between devices  11.4 us (6%)
  waiting for transfers between devices  8.96 us (5%)
  matrix products  6.22 us (3%)
  local copies, waits for them, and re-layouts  3.16 us (2%)
    pallas_call x1, Pallas kernels, spread(): pl.pallas_call(functools.partial(spread_kernel, groups, col_groups), name...  140 us
    all_to_all x1, waiting for transfers between devices, local(): back = lax.all_to_all(back, 'row', split_axis=0, concat_axis=0, tiled=True)  8.63 us
    all_to_all x1, starting transfers between devices, local(): lax.all_to_all(outgoing, 'row', split_axis=0, concat_axis=0, tiled=True)  7.38 us
    dot_general x4, matrix products, select(): lax.dot_general(one_hot.astype(values.dtype), values, (((left_axis,), (0,...  6.22 us
    all_to_all x1, starting transfers between devices, local(): back = lax.all_to_all(back, 'row', split_axis=0, concat_axis=0, tiled=True)  4.03 us
  transfers between devices with their start and end apart: 2, of which 2 were waited for; matrix products, arithmetic and copies ran while one was open for 7% of the time, Pallas kernels for 0%

profile of v5, /device:TPU:0, one launch (start us, length us, event | category | flops | bytes accessed | tf_op | source)
XLA Modules:
  0.0 184.5 jit_solution(5777215310394630687)
XLA Ops:
  0.6 0.0 copy-start.2
  0.6 0.8 add_select_fusion.1
  1.5 2.1 %select_reduce_fusion = s32[384]{0:T(512)S(1)} fusion(s32[6144]{0:T(1024)} %param.14, s32[384]{0:T(512)S(1)} %get-tuple-element.15), kind=kLoop, calls=%fused_computation | loop fusion | flops 7077504 | bytes 27648 | tf_op jit(solution)/shard_map/reduce_sum | solution.py:468
  3.6 0.3 convert_reduce_fusion
  3.9 2.0 %convolution_convert_fusion.1 = bf16[384,256]{1,0:T(8,128)(2,1)} fusion(bf16[384,256]{1,0:T(8,128)(2,1)} %param.8, s32[384]{0:T(512)S(1)} %multiply_add_fusion), kind=kOutput, calls=%fused_computation.3 | convolution fusion | flops 75743232 | bytes 394752 | tf_op jit(solution)/shard_map/dot_general | solution.py:433
  6.0 7.4 %all-to-all-start = ((bf16[16,24,256]{2,1,0:T(8,128)(2,1)}), bf16[16,24,256]{2,1,0:T(8,128)(2,1)S(1)}, u32[]{:S(2)}, u32[]{:S(2)}) async-start(bf16[16,24,256]{2,1,0:T(8,128)(2,1)} %bitcast), calls=%async_computation | async-start | bytes 393216 | tf_op jit(solution)/shard_map/all_to_all | solution.py:478
  13.4 1.1 fusion.3
  14.4 0.8 select_reduce_fusion.5
  15.2 0.7 fusion.12
  15.9 1.1 multiply_reduce_fusion
  17.0 0.1 compare_and_fusion
  17.1 0.7 pad_convert_fusion.member_ref
  17.8 1.8 pad_maximum_fusion.pair_ref
  19.6 1.2 select_reduce_fusion.1
  20.8 0.3 select_reduce_fusion.4
  21.1 0.6 select_maximum_fusion.stats_ref
  21.7 0.2 convert_reduce_fusion.1
  22.0 0.3 all-to-all-done
  22.3 0.3 convolution_convert_fusion
  22.6 0.0 copy-done.2
  22.6 0.8 pad_maximum_fusion.1.ph_ref
  23.4 0.6 pad.20.lengths_ref
  24.0 140.4 %spread.1 = (f32[384,512]{1,0:T(8,128)}, f32[384,512]{1,0:T(8,128)}, f32[8,128]{1,0:T(8,128)}) custom-call(bf16[384,512]{1,0:T(8,128)(2,1)} %pad_maximum_fusion.pair_ref, bf16[384,512]{1,0:T(8,128)(2,1)} %pad_maximum_fusion.1.ph_ref, f32[8,128]{1,0:T(8,128)} %select_maximum_fusion.stats_ref, f32[384,128]{1,0:T(8,128)} %pad_convert_fusion.member_ref, ...), custom_call_target="tpu_custom_call" | custom-call | tf_op jit(solution)/shard_map/spread/pallas_call | solution.py:386
  164.4 0.0 copy-start.1
  164.4 0.0 copy-start.3
  164.4 0.0 copy-start
  164.4 2.6 %fusion = f32[384,256]{1,0:T(8,128)} fusion(f32[384,512]{1,0:T(8,128)} %get-tuple-element.8, s32[384]{0:T(512)S(1)} %multiply_add_fusion.1), kind=kOutput, calls=%fused_computation.9 | convolution fusion | flops 453132288 | bytes 787968 | tf_op jit(solution)/shard_map/dot_general | solution.py:433
  167.0 4.0 %all-to-all-start.1 = ((f32[16,24,256]{2,1,0:T(8,128)}), f32[16,24,256]{2,1,0:T(8,128)S(1)}, u32[]{:S(2)}, u32[]{:S(2)}) async-start(f32[16,24,256]{2,1,0:T(8,128)} %bitcast.5), calls=%async_computation.1 | async-start | bytes 786432 | tf_op jit(solution)/shard_map/all_to_all | solution.py:528
  171.1 1.8 slice.26
  172.8 0.0 copy-done.1
  172.8 0.8 slice.25
  173.6 0.0 copy-done.3
  173.6 0.8 bitcast_divide_fusion
  174.4 0.2 select_reduce_fusion.2
  174.6 8.6 %all-to-all-done.1 = f32[16,24,256]{2,1,0:T(8,128)S(1)} async-done(((f32[16,24,256]{2,1,0:T(8,128)}), f32[16,24,256]{2,1,0:T(8,128)S(1)}, u32[]{:S(2)}, u32[]{:S(2)}) %all-to-all-start.1) | async-done | bytes 393248 | tf_op jit(solution)/shard_map/all_to_all | solution.py:528
  183.2 0.0 copy-done
  183.2 1.3 convolution_add_fusion
  (6 shorter events, 0.1 us)
Async XLA Ops:
  0.6 22.0 %copy-start.2 = (bf16[384,256]{1,0:T(8,128)(2,1)S(1)}, bf16[384,256]{1,0:T(8,128)(2,1)}, u32[]{:S(2)}) copy-start(bf16[384,256]{1,0:T(8,128)(2,1)} %param.10) | copy-start | bytes 589828
  6.0 16.3 %all-to-all-start = ((bf16[16,24,256]{2,1,0:T(8,128)(2,1)}), bf16[16,24,256]{2,1,0:T(8,128)(2,1)S(1)}, u32[]{:S(2)}, u32[]{:S(2)}) async-start(bf16[16,24,256]{2,1,0:T(8,128)(2,1)} %bitcast), calls=%async_computation | async-start | bytes 393216 | tf_op jit(solution)/shard_map/all_to_all | solution.py:478
  164.4 8.4 %copy-start.1 = (f32[384,512]{1,0:T(8,128)S(1)}, f32[384,512]{1,0:T(8,128)}, u32[]{:S(2)}) copy-start(f32[384,512]{1,0:T(8,128)} %get-tuple-element.6) | copy-start | bytes 2359300
  164.4 9.2 %copy-start.3 = (s32[48]{0:T(128)S(1)}, s32[48]{0:T(128)}, u32[]{:S(2)}) copy-start(s32[48]{0:T(128)} %param.15) | copy-start | bytes 580
  164.4 18.8 %copy-start = (bf16[384,256]{1,0:T(8,128)(2,1)S(1)}, bf16[384,256]{1,0:T(8,128)(2,1)}, u32[]{:S(2)}) copy-start(bf16[384,256]{1,0:T(8,128)(2,1)} %param.8) | copy-start | bytes 589828
  167.0 16.2 %all-to-all-start.1 = ((f32[16,24,256]{2,1,0:T(8,128)}), f32[16,24,256]{2,1,0:T(8,128)S(1)}, u32[]{:S(2)}, u32[]{:S(2)}) async-start(f32[16,24,256]{2,1,0:T(8,128)} %bitcast.5), calls=%async_computation.1 | async-start | bytes 786432 | tf_op jit(solution)/shard_map/all_to_all | solution.py:528

commit v6 on v5

--- a/solution.py
+++ b/solution.py
@@ -188,6 +188,7 @@
         keeping(a).start()
 
     place(0)
+    place(1)
 
     stats_here().wait()
     for d in range(1, col_groups):
@@ -319,10 +320,9 @@
         pltpu.make_async_copy(ham_hbm, ham, fetch_sem.at[1]),
         pltpu.make_async_copy(mult_g_hbm, mult_g, fetch_sem.at[2]),
     ]
-    lag = min(2, half)
+    lag = 1
 
     launch(0)
-    place(1)
     for fetch in fetches:
         fetch.start()
     pair_acc[...] = jnp.zeros_like(pair_acc)

time: 185 us -> 188 us (1.016)
  Pallas kernels: 140 us -> 143 us
    pallas_call x1, Pallas kernels: 140 us -> 143 us  [spread(): pl.pallas_call(functools.partial(spread_kernel, groups, col_groups), name...]
  transfers between devices with their start and end apart: 2 -> 2, of which waited for: 2 -> 2; matrix products, arithmetic and copies ran while one was open for 7% -> 6% of each run, Pallas kernels for 0% -> 0%
where the time goes in v6:
time: 188 us
  Pallas kernels  143 us (76%)
  other arithmetic  13.6 us (7%)
  starting transfers between devices  11.9 us (6%)
  waiting for transfers between devices  8.96 us (5%)
  matrix products  6.22 us (3%)
  local copies, waits for them, and re-layouts  3.16 us (2%)
    pallas_call x1, Pallas kernels, spread(): pl.pallas_call(functools.partial(spread_kernel, groups, col_groups), name...  143 us
    all_to_all x1, waiting for transfers between devices, local(): back = lax.all_to_all(back, 'row', split_axis=0, concat_axis=0, tiled=True)  8.63 us
    all_to_all x1, starting transfers between devices, local(): lax.all_to_all(outgoing, 'row', split_axis=0, concat_axis=0, tiled=True)  7.38 us
    dot_general x4, matrix products, select(): lax.dot_general(one_hot.astype(values.dtype), values, (((left_axis,), (0,...  6.22 us
    all_to_all x1, starting transfers between devices, local(): back = lax.all_to_all(back, 'row', split_axis=0, concat_axis=0, tiled=True)  4.48 us
  transfers between devices with their start and end apart: 2, of which 2 were waited for; matrix products, arithmetic and copies ran while one was open for 6% of the time, Pallas kernels for 0%

profile of v6, /device:TPU:0, one launch (start us, length us, event | category | flops | bytes accessed | tf_op | source)
XLA Modules:
  0.0 187.5 jit_solution(9925347201772659592)
XLA Ops:
  0.6 0.0 copy-start.2
  0.6 0.8 add_select_fusion.1
  1.5 2.1 %select_reduce_fusion = s32[384]{0:T(512)S(1)} fusion(s32[6144]{0:T(1024)} %param.14, s32[384]{0:T(512)S(1)} %get-tuple-element.15), kind=kLoop, calls=%fused_computation | loop fusion | flops 7077504 | bytes 27648 | tf_op jit(solution)/shard_map/reduce_sum | solution.py:468
  3.6 0.3 convert_reduce_fusion
  3.9 2.0 %convolution_convert_fusion.1 = bf16[384,256]{1,0:T(8,128)(2,1)} fusion(bf16[384,256]{1,0:T(8,128)(2,1)} %param.8, s32[384]{0:T(512)S(1)} %multiply_add_fusion), kind=kOutput, calls=%fused_computation.3 | convolution fusion | flops 75743232 | bytes 394752 | tf_op jit(solution)/shard_map/dot_general | solution.py:433
  6.0 7.4 %all-to-all-start = ((bf16[16,24,256]{2,1,0:T(8,128)(2,1)}), bf16[16,24,256]{2,1,0:T(8,128)(2,1)S(1)}, u32[]{:S(2)}, u32[]{:S(2)}) async-start(bf16[16,24,256]{2,1,0:T(8,128)(2,1)} %bitcast), calls=%async_computation | async-start | bytes 393216 | tf_op jit(solution)/shard_map/all_to_all | solution.py:478
  13.4 1.1 fusion.3
  14.4 0.8 select_reduce_fusion.5
  15.2 0.7 fusion.12
  15.9 1.1 multiply_reduce_fusion
  17.0 0.1 compare_and_fusion
  17.1 0.7 pad_convert_fusion.member_ref
  17.8 1.8 pad_maximum_fusion.pair_ref
  19.6 1.2 select_reduce_fusion.1
  20.8 0.3 select_reduce_fusion.4
  21.1 0.6 select_maximum_fusion.stats_ref
  21.7 0.2 convert_reduce_fusion.1
  22.0 0.3 all-to-all-done
  22.3 0.3 convolution_convert_fusion
  22.6 0.0 copy-done.2
  22.6 0.8 pad_maximum_fusion.1.ph_ref
  23.4 0.6 pad.20.lengths_ref
  24.0 143.0 %spread.1 = (f32[384,512]{1,0:T(8,128)}, f32[384,512]{1,0:T(8,128)}, f32[8,128]{1,0:T(8,128)}) custom-call(bf16[384,512]{1,0:T(8,128)(2,1)} %pad_maximum_fusion.pair_ref, bf16[384,512]{1,0:T(8,128)(2,1)} %pad_maximum_fusion.1.ph_ref, f32[8,128]{1,0:T(8,128)} %select_maximum_fusion.stats_ref, f32[384,128]{1,0:T(8,128)} %pad_convert_fusion.member_ref, ...), custom_call_target="tpu_custom_call" | custom-call | tf_op jit(solution)/shard_map/spread/pallas_call | solution.py:386
  167.0 0.0 copy-start.1
  167.0 0.0 copy-start.3
  167.0 0.0 copy-start
  167.0 2.6 %fusion = f32[384,256]{1,0:T(8,128)} fusion(f32[384,512]{1,0:T(8,128)} %get-tuple-element.8, s32[384]{0:T(512)S(1)} %multiply_add_fusion.1), kind=kOutput, calls=%fused_computation.9 | convolution fusion | flops 453132288 | bytes 787968 | tf_op jit(solution)/shard_map/dot_general | solution.py:433
  169.6 4.5 %all-to-all-start.1 = ((f32[16,24,256]{2,1,0:T(8,128)}), f32[16,24,256]{2,1,0:T(8,128)S(1)}, u32[]{:S(2)}, u32[]{:S(2)}) async-start(f32[16,24,256]{2,1,0:T(8,128)} %bitcast.5), calls=%async_computation.1 | async-start | bytes 786432 | tf_op jit(solution)/shard_map/all_to_all | solution.py:528
  174.1 1.8 slice.26
  175.8 0.0 copy-done.1
  175.8 0.8 slice.25
  176.6 0.0 copy-done.3
  176.6 0.8 bitcast_divide_fusion
  177.4 0.2 select_reduce_fusion.2
  177.6 8.6 %all-to-all-done.1 = f32[16,24,256]{2,1,0:T(8,128)S(1)} async-done(((f32[16,24,256]{2,1,0:T(8,128)}), f32[16,24,256]{2,1,0:T(8,128)S(1)}, u32[]{:S(2)}, u32[]{:S(2)}) %all-to-all-start.1) | async-done | bytes 393248 | tf_op jit(solution)/shard_map/all_to_all | solution.py:528
  186.2 0.0 copy-done
  186.2 1.3 convolution_add_fusion
  (6 shorter events, 0.1 us)
Async XLA Ops:
  0.6 22.0 %copy-start.2 = (bf16[384,256]{1,0:T(8,128)(2,1)S(1)}, bf16[384,256]{1,0:T(8,128)(2,1)}, u32[]{:S(2)}) copy-start(bf16[384,256]{1,0:T(8,128)(2,1)} %param.10) | copy-start | bytes 589828
  6.0 16.3 %all-to-all-start = ((bf16[16,24,256]{2,1,0:T(8,128)(2,1)}), bf16[16,24,256]{2,1,0:T(8,128)(2,1)S(1)}, u32[]{:S(2)}, u32[]{:S(2)}) async-start(bf16[16,24,256]{2,1,0:T(8,128)(2,1)} %bitcast), calls=%async_computation | async-start | bytes 393216 | tf_op jit(solution)/shard_map/all_to_all | solution.py:478
  167.0 8.9 %copy-start.1 = (f32[384,512]{1,0:T(8,128)S(1)}, f32[384,512]{1,0:T(8,128)}, u32[]{:S(2)}) copy-start(f32[384,512]{1,0:T(8,128)} %get-tuple-element.6) | copy-start | bytes 2359300
  167.0 9.6 %copy-start.3 = (s32[48]{0:T(128)S(1)}, s32[48]{0:T(128)}, u32[]{:S(2)}) copy-start(s32[48]{0:T(128)} %param.15) | copy-start | bytes 580
  167.0 19.2 %copy-start = (bf16[384,256]{1,0:T(8,128)(2,1)S(1)}, bf16[384,256]{1,0:T(8,128)(2,1)}, u32[]{:S(2)}) copy-start(bf16[384,256]{1,0:T(8,128)(2,1)} %param.8) | copy-start | bytes 589828
  169.6 16.7 %all-to-all-start.1 = ((f32[16,24,256]{2,1,0:T(8,128)}), f32[16,24,256]{2,1,0:T(8,128)S(1)}, u32[]{:S(2)}, u32[]{:S(2)}) async-start(f32[16,24,256]{2,1,0:T(8,128)} %bitcast.5), calls=%async_computation.1 | async-start | bytes 786432 | tf_op jit(solution)/shard_map/all_to_all | solution.py:528
